TPU v7x, 32 devices: a whole 2x2x4 slice. The times are simulated.
32 devices in a mesh: parts: 2 (over y), row: 4 (over z), col: 2 (over x), rhs: 2 (over core).
Axes of the slice: x: 2, y: 2, z: 4, core: 2. Of those that a mesh axis runs over, the one named last changes fastest.
Arguments:
- blocks: bfloat16 [8, 2, 96, 128, 128], P(('parts', 'row'), 'col'), parts along dimension 0, as said below
- block_rows: int32 [8, 2, 96], P(('parts', 'row'), 'col'), parts along dimension 0, may hold values from 0 to 127, as said below
- block_cols: int32 [8, 2, 96], P(('parts', 'row'), 'col'), parts along dimension 0, may hold values from 0 to 255, as said below
- counts: int32 [8, 2], P(('parts', 'row'), 'col'), parts along dimension 0, may hold values from 1 to 96, as said below
- diagonal: float32 [131072], P(('parts', 'row', 'col')), parts along dimension 0, may hold values from 1.2 to 4
- target: float32 [131072, 256], P(('parts', 'row', 'col'), 'rhs'), parts along dimension 0, may hold values from -6 to 6
Outputs:
- solution: float32 [131072, 256], P(('parts', 'row', 'col'), 'rhs'), parts along dimension 0
- residual: float32 [131072, 256], P(('parts', 'row', 'col'), 'rhs'), parts along dimension 0
There are 2 independent parts, one for each index of `parts`. A program takes and returns all parts, laid end to end along the dimension named above; each array names one. Nothing has to cross between parts.
Inputs may be any that keep to these rules, and one draw needn't show every extreme that they name: Each tile's used slots are its first counts slots; the busiest tile has exactly 96. `block_rows`: used slots of one tile name distinct blocks on or above the diagonal. `block_cols`: see block_rows. `blocks`: unused slots hold values that do not enter the operator; the operator is positive definite.
All inputs are finite; a program needn't handle non-finite values.
Results may differ from a plain program's by a relative error of at most 0.0045.
Values may be sent and summed in bfloat16 or wider, within the bound.
A program may use at most 128 MiB of HBM per device.

v0:
```python
import jax
import jax.numpy as jnp
from jax import lax
from jax.sharding import PartitionSpec as P

ITERS = 2


def one_hot_slots(indices, valid, extent):
    return ((indices[None, :] == jnp.arange(extent)[:, None]) & valid[None, :]).astype(jnp.float32)


def on_device(blocks, block_rows, block_cols, counts, diagonal, target):
    highest = lax.Precision.HIGHEST
    nrow = lax.axis_size("row")
    ncol = lax.axis_size("col")
    stored = blocks[0, 0]
    slots = stored.shape[0]
    width = stored.shape[1]
    local = target.shape[0]
    ncols = target.shape[1]
    quarter = local // width
    row_blocks = ncol * quarter
    col_blocks = nrow * quarter
    valid = jnp.arange(slots) < counts[0, 0]
    rows_hot = one_hot_slots(block_rows[0, 0], valid, row_blocks)
    cols_hot = one_hot_slots(block_cols[0, 0], valid, col_blocks)

    def squares(vector):
        return lax.psum(jnp.sum(vector * vector, axis=0), ("row", "col"))

    solution = jnp.zeros_like(target)
    residual = target
    direction = target
    norm_now = squares(residual)
    for step in range(ITERS):
        operate_field_low = direction.astype(jnp.bfloat16)
        direct_gathered = lax.all_gather(operate_field_low, "row", axis=0, tiled=True).reshape(
            col_blocks, width, ncols
        )
        prod = jnp.einsum(
            "kab,kbc->kac",
            stored,
            direct_gathered[block_cols[0, 0]],
            preferred_element_type=jnp.float32,
        )
        direct_partial_value = jnp.einsum("ik,kac->iac", rows_hot, prod, precision=highest)
        direct = lax.psum_scatter(
            direct_partial_value.reshape(row_blocks * width, ncols).astype(jnp.bfloat16),
            "col",
            scatter_dimension=0,
            tiled=True,
        ).astype(jnp.float32)
        gathered = lax.all_gather(operate_field_low, "col", axis=0, tiled=True).reshape(
            row_blocks, width, ncols
        )
        tprod = jnp.einsum(
            "kba,kbc->kac", stored, gathered[block_rows[0, 0]], preferred_element_type=jnp.float32
        )
        partial_value = jnp.einsum("jk,kac->jac", cols_hot, tprod, precision=highest)
        parcel = partial_value.astype(jnp.bfloat16).reshape(nrow, local, ncols)
        mirrored = jnp.sum(
            lax.all_to_all(parcel, "row", split_axis=0, concat_axis=0, tiled=True).astype(
                jnp.float32
            ),
            axis=0,
        )
        image = diagonal[:, None] * direction + direct + mirrored
        curve = lax.psum(jnp.sum(direction * image, axis=0), ("row", "col"))
        alpha = norm_now / curve
        solution = solution + alpha * direction
        residual = residual - alpha * image
        if step + 1 < ITERS:
            norm_next = squares(residual)
            direction = residual + norm_next / norm_now * direction
            norm_now = norm_next
    return (solution, residual)


def solution(mesh):
    return jax.shard_map(
        on_device,
        mesh=mesh,
        in_specs=(
            P(("parts", "row"), "col", None, None, None),
            P(("parts", "row"), "col", None),
            P(("parts", "row"), "col", None),
            P(("parts", "row"), "col"),
            P(("parts", "row", "col")),
            P(("parts", "row", "col"), "rhs"),
        ),
        out_specs=(P(("parts", "row", "col"), "rhs"), P(("parts", "row", "col"), "rhs")),
        check_vma=False,
    )
```

profile of v0, /device:TPU:12, one launch (start us, length us, event | category | flops | bytes accessed | tf_op | source)
XLA Modules:
  0.0 968.8 jit_solution(810773173325068209)
XLA Ops:
  7.2 0.0 all-gather.7.cloned.1.call-start
  7.2 3.9 convert_element_type.38
  11.1 0.0 all-gather.5.cloned.1.call-start
  11.2 0.7 all-gather.5.cloned.1.call-update
  12.6 56.6 %all-gather.7.cloned.1.call-done = bf16[16384,128]{1,0:T(8,128)(2,1)} async-done(((bf16[8192,128]{1,0:T(8,128)(2,1)}), bf16[16384,128]{1,0:T(8,128)(2,1)}) %all-gather.7.cloned.1.call-update) | async-done | bytes 4194320 | tf_op jit(solution)/shard_map/all_gather | solution.py:54
  69.1 4.9 gather_fusion.1
  74.0 6.1 fusion.10
  80.1 7.2 copy.13
  87.3 13.1 %convolution_convert_fusion.1 = bf16[256,128,128]{2,0,1:T(8,128)(2,1)} fusion(f32[96,128,128]{1,0,2:T(8,128)} %copy.13, s32[96]{0:T(128)S(1)} %bitcast.65, pred[96]{0:T(512)(128)(4,1)S(1)} %iota_compare_fusion.2), kind=kOutput, calls=%fused_computation.7 | convolution fusion | flops 4836081664 | bytes 14680544 | tf_op jit(solution)/shard_map/jk,kac->jac/dot_general | solution.py:60
  100.5 12.0 %copy.9 = bf16[256,128,128]{2,1,0:T(8,128)(2,1)} copy(bf16[256,128,128]{2,0,1:T(8,128)(2,1)} %convolution_convert_fusion.1) | data formatting | bytes 16777216 | tf_op jit(solution)/shard_map/convert_element_type | solution.py:61
  112.5 6.2 all-to-all-start
  118.7 0.4 reduce-scatter.3.cloned.1.call-start
  119.1 237.6 %all-gather.5.cloned.1.call-done = bf16[32768,128]{1,0:T(8,128)(2,1)} async-done(((bf16[8192,128]{1,0:T(8,128)(2,1)}), bf16[32768,128]{1,0:T(8,128)(2,1)}) %all-gather.5.cloned.1.call-update) | async-done | bytes 8388624 | tf_op jit(solution)/shard_map/all_gather | solution.py:38
  356.7 6.1 gather_fusion
  362.8 6.9 fusion.12
  369.7 6.6 copy.12
  376.3 7.1 fusion.14
  383.4 4.7 copy.8
  388.2 0.0 all-gather.11.cloned.1.call-start
  388.2 8.1 all-to-all-done
  396.3 7.4 convert_reduce_fusion.1
  403.7 41.2 %reduce-scatter.3.cloned.1.call-done = bf16[8192,128]{1,0:T(8,128)(2,1)} async-done(((bf16[16384,128]{1,0:T(8,128)(2,1)}), bf16[8192,128]{1,0:T(8,128)(2,1)}) %reduce-scatter.3.cloned.1.call-update) | async-done | bytes 2097168 | tf_op jit(solution)/shard_map/reduce_scatter | solution.py:48
  445.0 4.6 multiply_reduce_fusion.2
  449.6 17.7 %all-reduce = (f32[128]{0:T(128)S(1)}, f32[128]{0:T(128)S(1)}) all-reduce(f32[128]{0:T(128)S(1)} %get-tuple-element.3, f32[128]{0:T(128)S(1)} %get-tuple-element.2), channel_id=1, replica_groups=mesh['parts'=2,'row'=4,'col'=2,'rhs'=2] {'row','col'}, use_global_device_ids=true, to_apply=%region_1.0 | all-reduce | flops 256 | bytes 2048 | tf_op jit(solution)/shard_map/psum | solution.py:30
  467.3 5.9 multiply_reduce_fusion.1
  473.3 17.1 %psum.30 = f32[128]{0:T(128)S(1)} all-reduce(f32[128]{0:T(128)S(1)} %get-tuple-element.6), channel_id=1, replica_groups=mesh['parts'=2,'row'=4,'col'=2,'rhs'=2] {'row','col'}, use_global_device_ids=true, to_apply=%region_7.0 | all-reduce | flops 128 | bytes 1024 | tf_op jit(solution)/shard_map/psum | solution.py:30
  490.4 5.3 fusion.20
  495.7 0.0 all-gather.9.cloned.1.call-start
  495.8 0.5 all-gather.9.cloned.1.call-update
  496.3 57.7 %all-gather.11.cloned.1.call-done = bf16[16384,128]{1,0:T(8,128)(2,1)} async-done(((bf16[8192,128]{1,0:T(8,128)(2,1)}), bf16[16384,128]{1,0:T(8,128)(2,1)}) %all-gather.11.cloned.1.call-update) | async-done | bytes 4194320 | tf_op jit(solution)/shard_map/all_gather | solution.py:54
  554.0 4.9 gather_fusion.3
  558.9 6.2 fusion.6
  565.1 7.1 copy.15
  572.1 13.1 %convolution_convert_fusion = bf16[256,128,128]{2,0,1:T(8,128)(2,1)} fusion(f32[96,128,128]{1,0,2:T(8,128)} %copy.15, s32[96]{0:T(128)S(1)} %bitcast.66, pred[96]{0:T(512)(128)(4,1)S(1)} %iota_compare_fusion.2), kind=kOutput, calls=%fused_computation.6 | convolution fusion | flops 4836081664 | bytes 14680544 | tf_op jit(solution)/shard_map/jk,kac->jac/dot_general | solution.py:60
  585.3 12.0 %copy.11 = bf16[256,128,128]{2,1,0:T(8,128)(2,1)} copy(bf16[256,128,128]{2,0,1:T(8,128)(2,1)} %convolution_convert_fusion) | data formatting | bytes 16777216 | tf_op jit(solution)/shard_map/convert_element_type | solution.py:61
  597.3 6.2 all-to-all-start.1
  603.5 237.5 %all-gather.9.cloned.1.call-done = bf16[32768,128]{1,0:T(8,128)(2,1)} async-done(((bf16[8192,128]{1,0:T(8,128)(2,1)}), bf16[32768,128]{1,0:T(8,128)(2,1)}) %all-gather.9.cloned.1.call-update) | async-done | bytes 8388624 | tf_op jit(solution)/shard_map/all_gather | solution.py:38
  841.0 6.1 gather_fusion.2
  847.1 6.9 fusion.8
  854.0 6.8 copy.14
  860.8 7.1 fusion.17
  867.9 4.6 copy.10
  872.5 8.1 all-to-all-done.1
  880.6 7.5 convert_reduce_fusion
  888.0 41.3 %reduce-scatter.5.cloned.1.call-done = bf16[8192,128]{1,0:T(8,128)(2,1)} async-done(((bf16[16384,128]{1,0:T(8,128)(2,1)}), bf16[8192,128]{1,0:T(8,128)(2,1)}) %reduce-scatter.5.cloned.1.call-update) | async-done | bytes 2097168 | tf_op jit(solution)/shard_map/reduce_scatter | solution.py:48
  929.3 5.9 multiply_reduce_fusion
  935.2 17.7 %psum.31 = f32[128]{0:T(128)S(1)} all-reduce(f32[128]{0:T(128)S(1)} %multiply_reduce_fusion), channel_id=1, replica_groups=mesh['parts'=2,'row'=4,'col'=2,'rhs'=2] {'row','col'}, use_global_device_ids=true, to_apply=%region_11.0 | all-reduce | flops 128 | bytes 1024 | tf_op jit(solution)/shard_map/psum | solution.py:69
  953.0 8.7 multiply_subtract_fusion
  (21 shorter events, 0.1 us)
Async XLA Ops:
  7.2 66.9 %copy-start = (bf16[1,1,96,128,128]{4,3,2,1,0:T(8,128)(2,1)S(1)}, bf16[1,1,96,128,128]{4,3,2,1,0:T(8,128)(2,1)}, u32[]{:S(2)}) copy-start(bf16[1,1,96,128,128]{4,3,2,1,0:T(8,128)(2,1)} %param.6) | copy-start | bytes 9437188
  7.2 5.4 copy-start.3
  7.2 61.9 %all-gather.7.cloned.1.call-start = ((), (), s32[]{:S(2)}) async-start(), calls=%async_computation.6 | async-start | bytes 6291456 | tf_op jit(solution)/shard_map/all_gather | solution.py:54
  11.1 345.6 %all-gather.5.cloned.1.call-start = ((), (), s32[]{:S(2)}) async-start(), calls=%async_computation.4 | async-start | bytes 10485760 | tf_op jit(solution)/shard_map/all_gather | solution.py:38
  80.1 7.2 copy-start.2
  112.5 283.9 %all-to-all-start = ((bf16[4,8192,128]{2,1,0:T(8,128)(2,1)}), bf16[4,8192,128]{2,1,0:T(8,128)(2,1)}, u32[]{:S(2)}, u32[]{:S(2)}) async-start(bf16[4,8192,128]{2,1,0:T(8,128)(2,1)} %bitcast.57), calls=%async_computation.1 | async-start | bytes 16777216 | tf_op jit(solution)/shard_map/all_to_all | solution.py:63
  118.7 326.3 %reduce-scatter.3.cloned.1.call-start = ((), (), s32[]{:S(2)}) async-start(), calls=%async_computation.5 | async-start | bytes 6291456 | tf_op jit(solution)/shard_map/reduce_scatter | solution.py:48
  388.1 56.8 %copy-start.1 = (f32[8192]{0:T(1024)S(1)}, f32[8192]{0:T(1024)}, u32[]{:S(2)}) copy-start(f32[8192]{0:T(1024)} %param.10) | copy-start | bytes 98308
  388.2 165.9 %all-gather.11.cloned.1.call-start = ((), (), s32[]{:S(2)}) async-start(), calls=%async_computation.9 | async-start | bytes 6291456 | tf_op jit(solution)/shard_map/all_gather | solution.py:54
  495.7 345.3 %all-gather.9.cloned.1.call-start = ((), (), s32[]{:S(2)}) async-start(), calls=%async_computation.7 | async-start | bytes 10485760 | tf_op jit(solution)/shard_map/all_gather | solution.py:38
  597.3 283.3 %all-to-all-start.1 = ((bf16[4,8192,128]{2,1,0:T(8,128)(2,1)}), bf16[4,8192,128]{2,1,0:T(8,128)(2,1)}, u32[]{:S(2)}, u32[]{:S(2)}) async-start(bf16[4,8192,128]{2,1,0:T(8,128)(2,1)} %bitcast.58), calls=%async_computation.3 | async-start | bytes 16777216 | tf_op jit(solution)/shard_map/all_to_all | solution.py:63
  603.5 325.9 %reduce-scatter.5.cloned.1.call-start = ((), (), s32[]{:S(2)}) async-start(), calls=%async_computation.8 | async-start | bytes 6291456 | tf_op jit(solution)/shard_map/reduce_scatter | solution.py:48
Sparse Core Ops, SparseCore 0:
  11.2 57.8 all-gather.6
  71.3 285.4 all-gather.4
  388.3 56.6 reduce-scatter.2
  495.8 58.1 all-gather.10
  555.5 285.4 all-gather.8
  872.6 56.6 reduce-scatter.4
where the time goes:
time: 976 us; the launch traced here: 969 us
  waiting for transfers between devices  689 us (71%)
  local copies, waits for them, and re-layouts  83.1 us (9%)
  matrix products  66.4 us (7%)
  blocking collectives  52.6 us (5%)
  other arithmetic  49.3 us (5%)
  between operations  15.1 us (2%)
  starting transfers between devices  13 us (1%)
    all_gather x2, waiting for transfers between devices, on_device(): lax.all_gather(operate_field_low, 'row', axis=0, tiled=True)  475 us
    all_gather x2, waiting for transfers between devices, on_device(): lax.all_gather(operate_field_low, 'col', axis=0, tiled=True)  114 us
    reduce_scatter x2, waiting for transfers between devices, on_device(): lax.psum_scatter(direct_partial_value.reshape(row_blocks * width, ncols)....  82.5 us
    psum x2, blocking collectives, squares(): return lax.psum(jnp.sum(vector * vector, axis=0), ('row', 'col'))  34.8 us
    dot_general x2, matrix products, on_device(): jnp.einsum('jk,kac->jac', cols_hot, tprod, precision=highest)  26.2 us
    convert_element_type x2, local copies, waits for them, and re-layouts, on_device(): parcel = partial_value.astype(jnp.bfloat16).reshape(nrow, local, ncols)  24 us
  transfers between devices with their start and end apart: 8, of which 8 were waited for; matrix products, arithmetic and copies ran while one was open for 17% of the time, Pallas kernels for 0%

commit v1 on v0

--- a/solution.py
+++ b/solution.py
@@ -1,9 +1,132 @@
+import functools
 import jax
 import jax.numpy as jnp
 from jax import lax
+from jax.experimental import pallas as pl
+from jax.experimental.pallas import tpu as pltpu
 from jax.sharding import PartitionSpec as P
 
 ITERS = 2
+UNROLL = 8
+GATHER_BYTES = 32 * 2**20
+
+
+def operate_kernel(slots, irow_ref, icol_ref, count_ref, blocks_ref, low_ref, image_ref):
+    tile = pl.program_id(0)
+
+    @pl.when(tile == 0)
+    def _():
+        image_ref[...] = jnp.zeros_like(image_ref)
+
+    count = count_ref[tile]
+
+    def group(step, carry):
+        base = step * UNROLL
+        terms = []
+        for u in range(UNROLL):
+            k = base + u
+            i = irow_ref[tile * slots + k]
+            j = icol_ref[tile * slots + k]
+            block = blocks_ref[0, k]
+            direct = lax.dot_general(
+                low_ref[j], block, (((1,), (1,)), ((), ())), preferred_element_type=jnp.float32
+            )
+            mirrored = lax.dot_general(
+                low_ref[i], block, (((1,), (0,)), ((), ())), preferred_element_type=jnp.float32
+            )
+            terms.append((k < count, i, j, direct, mirrored))
+        for used, i, j, direct, mirrored in terms:
+            image_ref[i] += jnp.where(used, direct, 0.0)
+            image_ref[j] += jnp.where(used, mirrored, 0.0)
+        return carry
+
+    lax.fori_loop(0, (count + UNROLL - 1) // UNROLL, group, 0)
+
+
+def operate(blocks, irow, icol, count, low):
+    tiles, slots, width, _ = blocks.shape
+    return pl.pallas_call(
+        functools.partial(operate_kernel, slots),
+        out_shape=jax.ShapeDtypeStruct(low.shape, jnp.float32),
+        grid_spec=pltpu.PrefetchScalarGridSpec(
+            num_scalar_prefetch=3,
+            grid=(tiles,),
+            in_specs=[
+                pl.BlockSpec((1, slots, width, width), lambda t, *_: (t, 0, 0, 0)),
+                pl.BlockSpec(low.shape, lambda t, *_: (0, 0, 0)),
+            ],
+            out_specs=pl.BlockSpec(low.shape, lambda t, *_: (0, 0, 0)),
+        ),
+        compiler_params=pltpu.CompilerParams(vmem_limit_bytes=40 * 2**20),
+    )(irow, icol, count, blocks, low)
+
+
+def by_columns(blocks, block_rows, block_cols, counts, diagonal, target):
+    grid = ("row", "col")
+    nrow = lax.axis_size("row")
+    ncol = lax.axis_size("col")
+    nrhs = lax.axis_size("rhs")
+    devices = nrow * ncol
+    stored = blocks[0, 0]
+    slots, width, _ = stored.shape
+    quarter = target.shape[0] // width
+    own = target.shape[1] // devices
+    row_blocks = ncol * quarter
+
+    half = slots // nrhs
+    piece = lax.dynamic_slice_in_dim(stored, lax.axis_index("rhs") * half, half, axis=0)
+    tiles = lax.all_gather(piece, grid, axis=0, tiled=False)
+    tiles = lax.all_gather(tiles, "rhs", axis=0, tiled=False)
+    tiles = tiles.reshape(nrhs * devices, half, width, width)
+
+    row, col = lax.axis_index("row"), lax.axis_index("col")
+    irow = row * row_blocks + block_rows[0, 0]
+    jcol = block_cols[0, 0]
+    icol = (jcol // quarter * ncol + col) * quarter + jcol % quarter
+    names = jnp.concatenate([irow, icol, counts[0]])
+    names = lax.all_gather(names, grid, axis=0, tiled=False)
+
+    def halves(index):
+        return index.reshape(devices, nrhs, half).transpose(1, 0, 2).reshape(-1)
+
+    rows_all = halves(names[:, :slots])
+    cols_all = halves(names[:, slots : 2 * slots])
+    count = names[:, 2 * slots]
+    count_all = jnp.clip(
+        count[None, :] - jnp.arange(nrhs, dtype=jnp.int32)[:, None] * half, 0, half
+    ).reshape(-1)
+
+    diag = lax.all_gather(diagonal, grid, axis=0, tiled=True).reshape(-1, 1, width)
+
+    def outward(field):
+        parcel = field.reshape(quarter, width, devices, own).transpose(2, 0, 3, 1)
+        return lax.all_to_all(parcel, grid, split_axis=0, concat_axis=0, tiled=True).reshape(
+            devices * quarter, own, width
+        )
+
+    def inner(a, b):
+        return jnp.sum(a * b, axis=(0, 2), keepdims=True)
+
+    residual = outward(target)
+    direction = residual
+    answer = jnp.zeros_like(residual)
+    norm_now = inner(residual, residual)
+    for step in range(ITERS):
+        product = operate(tiles, rows_all, cols_all, count_all, direction.astype(jnp.bfloat16))
+        image = diag * direction + product
+        alpha = norm_now / inner(direction, image)
+        answer = answer + alpha * direction
+        residual = residual - alpha * image
+        if step + 1 < ITERS:
+            norm_next = inner(residual, residual)
+            direction = residual + norm_next / norm_now * direction
+            norm_now = norm_next
+    both = jnp.stack([answer, residual]).astype(jnp.bfloat16)
+    parcel = both.reshape(2, devices, quarter, own, width)
+    home = lax.all_to_all(parcel, grid, split_axis=1, concat_axis=1, tiled=True)
+    home = home.transpose(0, 2, 4, 1, 3).reshape(2, quarter * width, devices * own)
+    home = home.astype(jnp.float32)
+    return (home[0], home[1])
 
 
 def one_hot_slots(indices, valid, extent):
@@ -14,6 +137,13 @@
     highest = lax.Precision.HIGHEST
     nrow = lax.axis_size("row")
     ncol = lax.axis_size("col")
+    tile_bytes = blocks[0, 0].size * blocks.dtype.itemsize
+    if (
+        nrow * ncol * tile_bytes <= GATHER_BYTES
+        and target.shape[1] % (16 * nrow * ncol) == 0
+        and blocks.shape[2] % (UNROLL * lax.axis_size("rhs")) == 0
+    ):
+        return by_columns(blocks, block_rows, block_cols, counts, diagonal, target)
     stored = blocks[0, 0]
     slots = stored.shape[0]
     width = stored.shape[1]

time: 976 us -> 541 us (0.55)
  waiting for transfers between devices: 689 us -> 176 us
  blocking collectives: 52.6 us -> 212 us
  matrix products: 66.4 us -> 0 us
  Pallas kernels: 0 us -> 64.9 us
  other arithmetic: 49.3 us -> 13.1 us
  local copies, waits for them, and re-layouts: 83.1 us -> 48.7 us
    all_gather x4 -> x2, waiting for transfers between devices: 589 us -> 176 us  [the longest x1 176 us: by_columns(): tiles = lax.all_gather(piece, grid, axis=0, tiled=False)]
    all_to_all x0 -> x1, blocking collectives: none -> 92.9 us  [by_columns(): home = lax.all_to_all(parcel, grid, split_axis=1, concat_axis=1, tiled=True)]
    unnamed x0 -> x1, blocking collectives: none -> 88.7 us
    reduce_scatter x2 -> x0, waiting for transfers between devices: 82.5 us -> none  [on_device(): lax.psum_scatter(direct_partial_value.reshape(row_blocks * width, ncols)....]
    dot_general x8 -> x0, matrix products: 66.4 us -> none  [the longest x2 26.2 us: on_device(): jnp.einsum('jk,kac->jac', cols_hot, tprod, precision=highest)]
    pallas_call x0 -> x2, Pallas kernels: none -> 64.9 us  [operate(): pl.pallas_call(functools.partial(operate_kernel, slots), out_shape=jax.Sh...]
    psum x3 -> x0, blocking collectives: 52.6 us -> none  [the longest x2 34.8 us: squares(): return lax.psum(jnp.sum(vector * vector, axis=0), ('row', 'col'))]
    unnamed x8 -> x24, local copies, waits for them, and re-layouts: 0.02 us -> 37.7 us
  transfers between devices with their start and end apart: 8 -> 3, of which waited for: 8 -> 1; matrix products, arithmetic and copies ran while one was open for 17% -> 4% of each run, Pallas kernels for 0% -> 0%
where the time goes in v1:
time: 541 us; the launch traced here: 539 us
  blocking collectives  212 us (39%)
  waiting for transfers between devices  176 us (33%)
  Pallas kernels  64.9 us (12%)
  local copies, waits for them, and re-layouts  48.7 us (9%)
  between operations  15.6 us (3%)
  other arithmetic  13.1 us (2%)
  starting transfers between devices  8.48 us (2%)
    all_gather x1, waiting for transfers between devices, by_columns(): tiles = lax.all_gather(piece, grid, axis=0, tiled=False)  176 us
    all_to_all x1, blocking collectives, by_columns(): home = lax.all_to_all(parcel, grid, split_axis=1, concat_axis=1, tiled=True)  92.9 us
    unnamed x1, blocking collectives  88.7 us
    pallas_call x2, Pallas kernels, operate(): pl.pallas_call(functools.partial(operate_kernel, slots), out_shape=jax.Sh...  64.9 us
    unnamed x24, local copies, waits for them, and re-layouts  37.7 us
    all_gather x1, blocking collectives, by_columns(): lax.all_gather(diagonal, grid, axis=0, tiled=True).reshape(-1, 1, width)  30.3 us
  transfers between devices with their start and end apart: 3, of which 1 were waited for; matrix products, arithmetic and copies ran while one was open for 4% of the time, Pallas kernels for 0%

profile of v1, /device:TPU:12, one launch (start us, length us, event | category | flops | bytes accessed | tf_op | source)
XLA Modules:
  0.0 538.8 jit_solution(15691602452316466473)
XLA Ops:
  7.2 0.0 copy-start
  7.2 0.0 all-gather.6.cloned.1.call-start
  7.2 1.8 copy-done
  9.1 1.3 constant_dynamic-slice_fusion
  10.4 0.0 all-gather.6.cloned.1.call-update
  10.4 0.0 all-gather.8.cloned.1.call-start
  10.5 176.1 %all-gather.6.cloned.1.call-done = bf16[8,1,48,128,128]{4,3,2,1,0:T(8,128)(2,1)} async-done(((bf16[1,1,48,128,128]{4,3,2,1,0:T(8,128)(2,1)}), bf16[8,1,48,128,128]{4,3,2,1,0:T(8,128)(2,1)}) %all-gather.6.cloned.1.call-update) | async-done | bytes 12582928 | tf_op jit(solution)/shard_map/all_gather | solution.py:78
  186.5 0.0 all-gather.8.cloned.1.call-update
  186.5 5.6 %copy.30 = f32[8192,128]{0,1:T(8,128)} copy(f32[8192,128]{1,0:T(8,128)} %param.11) | data formatting | bytes 8388608 | tf_op args[5]
  192.1 5.8 %copy.38 = f32[16,8,64,128]{3,2,1,0:T(8,128)} copy(f32[16,8,64,128]{3,1,2,0:T(8,128)} %bitcast.91) | data formatting | bytes 8388608
  197.9 8.4 %all-to-all-start = ((f32[8,64,16,128]{3,1,2,0:T(8,128)}), f32[8,64,16,128]{3,1,2,0:T(8,128)}, u32[]{:S(2)}, u32[]{:S(2)}) async-start(f32[8,64,16,128]{3,1,2,0:T(8,128)} %bitcast.88), calls=%async_computation | async-start | bytes 8388608 | tf_op jit(solution)/shard_map/all_to_all | solution.py:103
  207.0 0.6 dynamic-slice.1
  208.3 0.2 add_dynamic-update-slice_fusion
  208.5 88.7 %all-reduce = s32[1544]{0:T(1024)S(1)} all-reduce(s32[1544]{0:T(1024)S(1)} %add_dynamic-update-slice_fusion), channel_id=2, replica_groups=mesh['parts'=2,'row'=4,'col'=2,'rhs'=2] {'row','col'}, use_global_device_ids=true, to_apply=%add | all-reduce | flops 1544 | bytes 12352
  297.2 0.1 reshape.82
  297.3 0.2 slice_reduce_fusion
  297.5 0.1 subtract_clamp_fusion
  297.6 0.1 min.12.count_ref
  297.7 0.1 fusion.8
  297.7 0.1 reshape.79
  297.8 0.1 reshape.80.icol_ref
  297.9 0.1 reshape.77
  298.0 0.1 reshape.78.irow_ref
  298.1 30.3 %all_gather.21 = f32[65536]{0:T(1024)S(1)} all-gather(f32[8192]{0:T(1024)S(1)} %copy-done.4), channel_id=1, replica_groups=mesh['parts'=2,'row'=4,'col'=2,'rhs'=2] {'row','col'}, dimensions={0}, use_global_device_ids=true | all-gather | bytes 294912 | tf_op jit(solution)/shard_map/all_gather | solution.py:99
  328.4 0.0 all-to-all-done
  328.4 4.6 copy.31
  333.0 0.0 copy-start.2
  333.0 4.1 multiply_reduce_fusion.2
  337.1 0.3 bitcast_convert_fusion.low_ref
  337.4 0.0 all-gather.8.cloned.1.call-done
  337.4 0.0 copy-start.3
  337.4 32.6 %shard_map.77 = f32[512,16,128]{2,1,0:T(8,128)S(1)} custom-call(s32[768]{0:T(1024)S(1)} %reshape.78.irow_ref, s32[768]{0:T(1024)S(1)} %reshape.80.icol_ref, s32[16]{0:T(128)S(1)} %min.12.count_ref, bf16[16,48,128,128]{3,2,1,0:T(8,128)(2,1)} %bitcast.86, bf16[512,16,128]{2,1,0:T(8,128)(2,1)S(1)} %bitcast_convert_fusion.low_ref), custom_call_target="tpu_custom_call" | custom-call | tf_op jit(solution)/shard_map/pallas_call | solution.py:48
  370.1 0.7 fusion.1
  370.8 1.2 multiply_reduce_fusion.1
  371.9 1.1 fusion.6.low_ref
  373.0 32.3 %shard_map.78 = f32[512,16,128]{2,1,0:T(8,128)S(1)} custom-call(s32[768]{0:T(1024)S(1)} %reshape.78.irow_ref, s32[768]{0:T(1024)S(1)} %reshape.80.icol_ref, s32[16]{0:T(128)S(1)} %min.12.count_ref, bf16[16,48,128,128]{3,2,1,0:T(8,128)(2,1)} %bitcast.87, bf16[512,16,128]{2,1,0:T(8,128)(2,1)S(1)} %fusion.6.low_ref), custom_call_target="tpu_custom_call" | custom-call | tf_op jit(solution)/shard_map/pallas_call | solution.py:48
  405.3 1.5 multiply_reduce_fusion
  406.9 2.6 fusion.3
  409.4 0.5 copy.34
  410.0 0.5 copy.35
  410.5 0.4 pad_maximum_fusion
  410.9 92.9 %all_to_all.10 = bf16[2,8,64,16,128]{4,2,3,0,1:T(8,128)(2,1)S(1)} all-to-all(bf16[2,8,64,16,128]{4,2,3,0,1:T(8,128)(2,1)S(1)} %pad_maximum_fusion), channel_id=1, replica_groups=mesh['parts'=2,'row'=4,'col'=2,'rhs'=2] {'row','col'}, dimensions={1} | all-to-all | bytes 8388608 | tf_op jit(solution)/shard_map/all_to_all | solution.py:126
  503.8 1.0 convert_bitcast_fusion
  504.8 3.3 fusion.7
  508.1 5.2 copy.45
  513.3 5.6 %copy.37 = f32[8192,128]{1,0:T(8,128)} copy(f32[8192,128]{0,1:T(8,128)} %bitcast.89) | data formatting | bytes 8388608
  518.9 7.4 %copy.46 = f32[16,8,64,128]{3,1,2,0:T(8,128)} copy(f32[16,8,64,128]{3,2,1,0:T(8,128)} %bitcast.92) | data formatting | bytes 8388608
  526.3 5.7 %copy.36 = f32[8192,128]{1,0:T(8,128)} copy(f32[8192,128]{0,1:T(8,128)} %bitcast.90) | data formatting | bytes 8388608
  (21 shorter events, 0.1 us)
Async XLA Ops:
  7.2 1.9 copy-start
  7.2 179.3 %all-gather.6.cloned.1.call-start = ((), (), s32[]{:S(2)}) async-start(), calls=%async_computation.2 | async-start | bytes 14155776 | tf_op jit(solution)/shard_map/all_gather | solution.py:78
  10.4 327.0 %all-gather.8.cloned.1.call-start = ((), (), s32[]{:S(2)}) async-start(), calls=%async_computation.3 | async-start | bytes 37748736 | tf_op jit(solution)/shard_map/all_gather | solution.py:79
  197.9 9.1 %copy-start.7 = (u32[32]{0:T(128)S(1)}, u32[32]{0:T(128)}, u32[]{:S(2)}) copy-start(u32[32]{0:T(128)} %constant.59) | copy-start | bytes 388
  197.9 10.3 %copy-start.5 = (s32[1,1,96]{2,1,0:T(1,128)S(1)}, s32[1,1,96]{2,1,0:T(1,128)}, u32[]{:S(2)}) copy-start(s32[1,1,96]{2,1,0:T(1,128)} %param.8) | copy-start | bytes 1156
  197.9 10.4 %copy-start.6 = (s32[1,1,96]{2,1,0:T(1,128)S(1)}, s32[1,1,96]{2,1,0:T(1,128)}, u32[]{:S(2)}) copy-start(s32[1,1,96]{2,1,0:T(1,128)} %param.7) | copy-start | bytes 1156
  197.9 100.1 %copy-start.4 = (f32[8192]{0:T(1024)S(1)}, f32[8192]{0:T(1024)}, u32[]{:S(2)}) copy-start(f32[8192]{0:T(1024)} %param.10) | copy-start | bytes 98308
  197.9 130.4 %all-to-all-start = ((f32[8,64,16,128]{3,1,2,0:T(8,128)}), f32[8,64,16,128]{3,1,2,0:T(8,128)}, u32[]{:S(2)}, u32[]{:S(2)}) async-start(f32[8,64,16,128]{3,1,2,0:T(8,128)} %bitcast.88), calls=%async_computation | async-start | bytes 8388608 | tf_op jit(solution)/shard_map/all_to_all | solution.py:103
  333.0 4.1 copy-start.2
  337.4 32.6 %copy-start.3 = (f32[8,64,16,128]{3,2,1,0:T(8,128)S(1)}, f32[8,64,16,128]{3,2,1,0:T(8,128)}, u32[]{:S(2)}) copy-start(f32[8,64,16,128]{3,2,1,0:T(8,128)} %copy-done.2) | copy-start | bytes 12582916
  526.3 5.7 %copy-start.1 = (bf16[1,1,96,128,128]{4,3,2,1,0:T(8,128)(2,1)S(1)}, bf16[1,1,96,128,128]{4,3,2,1,0:T(8,128)(2,1)}, u32[]{:S(2)}) copy-start(bf16[1,1,96,128,128]{4,3,2,1,0:T(8,128)(2,1)} %param.6) | copy-start | bytes 9437188
Sparse Core Ops, SparseCore 0:
  10.8 175.6 all-gather.5
  188.1 40.5 all-gather.7

commit v2 on v0

--- a/solution.py
+++ b/solution.py
@@ -1,9 +1,325 @@
+import functools
 import jax
 import jax.numpy as jnp
 from jax import lax
+from jax.experimental import pallas as pl
+from jax.experimental.pallas import tpu as pltpu
 from jax.sharding import PartitionSpec as P
 
 ITERS = 2
+UNROLL = 8
+GATHER_BYTES = 32 * 2**20
+MESH = pl.DeviceIdType.MESH
+ANY = pl.BlockSpec(memory_space=pl.ANY)
+
+
+def spread_kernel(
+    nrow, stored, parcel, names, diag,
+    tiles, field, all_names, all_diag,
+    ring_send, ring_recv, send, recv, own_sem,
+):
+    devices = 2 * nrow
+    row, col, core = lax.axis_index("row"), lax.axis_index("col"), lax.axis_index("rhs")
+    me = row * 2 + col
+    place = jnp.where(col == 0, row, devices - 1 - row)
+
+    def device_at(place):
+        place = lax.rem(place + devices, devices)
+        back = place >= nrow
+        return jnp.where(back, devices - 1 - place, place), jnp.where(back, 1, 0)
+
+    def peer(offset):
+        other = lax.rem(me + offset, devices)
+        return {"row": other // 2, "col": lax.rem(other, 2)}
+
+    barrier = pltpu.get_barrier_semaphore()
+    for offset in range(1, devices):
+        pl.semaphore_signal(barrier, inc=1, device_id=peer(offset), device_id_type=MESH)
+    pl.semaphore_wait(barrier, devices - 1)
+
+    half = tiles.shape[1]
+    quart = half // 2
+    hops = []
+
+    def hop(way, step):
+        r, c = device_at(place + (1 if way == 0 else -1))
+        if step == 0:
+            source = stored.at[pl.ds(way * quart, quart), core]
+            origin = me
+        else:
+            orow, ocol = device_at(place + (-step if way == 0 else step))
+            origin = orow * 2 + ocol
+            source = tiles.at[origin, pl.ds(way * quart, quart)]
+        copy = pltpu.make_async_remote_copy(
+            src_ref=source,
+            dst_ref=tiles.at[origin, pl.ds(way * quart, quart)],
+            send_sem=ring_send.at[way, step],
+            recv_sem=ring_recv.at[way, step],
+            device_id={"row": r, "col": c},
+            device_id_type=MESH,
+        )
+        copy.start()
+        return copy
+
+    now = [hop(0, 0), hop(1, 0)]
+    straight = []
+    pairs = ((names, all_names, False), (diag, all_diag, False), (parcel, field, True))
+    for n, (source, target, apart) in enumerate(pairs):
+        for offset in range(1, devices):
+            copy = pltpu.make_async_remote_copy(
+                src_ref=source.at[lax.rem(me + offset, devices)] if apart else source,
+                dst_ref=target.at[me],
+                send_sem=send.at[n, offset - 1],
+                recv_sem=recv.at[n, offset - 1],
+                device_id=peer(offset),
+                device_id_type=MESH,
+            )
+            copy.start()
+            straight.append(copy)
+    local = []
+    owns = (
+        (stored.at[:, core], tiles.at[me]),
+        (names, all_names.at[me]),
+        (diag, all_diag.at[me]),
+        (parcel.at[me], field.at[me]),
+    )
+    for n, (source, target) in enumerate(owns):
+        copy = pltpu.make_async_copy(source, target, own_sem.at[n])
+        copy.start()
+        local.append(copy)
+    for step in range(1, devices):
+        for way in range(2):
+            now[way].wait_recv()
+            if step < devices - 1:
+                hops.append(now[way])
+                now[way] = hop(way, step)
+    hops += now
+    for copy in hops:
+        copy.wait_send()
+    for copy in straight:
+        copy.wait()
+    for copy in local:
+        copy.wait()
+
+
+def spread(stored, parcel, names, diag):
+    nrow = lax.axis_size("row")
+    devices = 2 * nrow
+    half, cores, width, _ = stored.shape
+    return pl.pallas_call(
+        functools.partial(spread_kernel, nrow),
+        out_shape=(
+            jax.ShapeDtypeStruct((devices, half, width, width), stored.dtype),
+            jax.ShapeDtypeStruct(parcel.shape, parcel.dtype),
+            jax.ShapeDtypeStruct((devices,) + names.shape, names.dtype),
+            jax.ShapeDtypeStruct((devices,) + diag.shape, diag.dtype),
+        ),
+        in_specs=[ANY] * 4,
+        out_specs=[ANY] * 4,
+        scratch_shapes=[
+            pltpu.SemaphoreType.DMA((2, devices - 1)),
+            pltpu.SemaphoreType.DMA((2, devices - 1)),
+            pltpu.SemaphoreType.DMA((3, devices - 1)),
+            pltpu.SemaphoreType.DMA((3, devices - 1)),
+            pltpu.SemaphoreType.DMA((4,)),
+        ],
+        compiler_params=pltpu.CompilerParams(collective_id=0, has_side_effects=True),
+    )(stored, parcel, names, diag)
+
+
+def pack_kernel(target_ref, parcel_ref):
+    devices, blocks, own, width = parcel_ref.shape
+    for b in range(blocks):
+        low = target_ref[b].T.astype(jnp.bfloat16)
+        parcel_ref[:, b] = low.reshape(devices, own, width)
+
+
+def pack(target, devices):
+    blocks, width, columns = target.shape
+    own = columns // devices
+    step = min(8, blocks)
+    return pl.pallas_call(
+        pack_kernel,
+        out_shape=jax.ShapeDtypeStruct((devices, blocks, own, width), jnp.bfloat16),
+        grid=(blocks // step,),
+        in_specs=[pl.BlockSpec((step, width, columns), lambda g: (g, 0, 0))],
+        out_specs=pl.BlockSpec((devices, step, own, width), lambda g: (0, g, 0, 0)),
+    )(target)
+
+
+def finish_kernel(target_ref, diag_ref, first_ref, second_ref, scale_ref, answer_ref, residual_ref):
+    blocks, width, columns = target_ref.shape
+    alpha1, alpha2, beta = scale_ref[0:1], scale_ref[1:2], scale_ref[2:3]
+    for b in range(blocks):
+        target = target_ref[b]
+        diag = jnp.transpose(jnp.broadcast_to(diag_ref[pl.ds(b, 1), :], (columns, width)))
+        first = first_ref[:, b].reshape(columns, width).astype(jnp.float32).T
+        second = second_ref[:, b].reshape(columns, width).astype(jnp.float32).T
+        lost = target - target.astype(jnp.bfloat16).astype(jnp.float32)
+        lost1 = lost - alpha1 * diag * lost
+        answer_ref[b] = alpha1 * target + alpha2 * (first + lost1 + beta * target)
+        residual_ref[b] = second + lost1 - alpha2 * diag * (lost1 + beta * lost)
+
+
+def finish(target, diag, first, second, scales):
+    blocks, width, columns = target.shape
+    devices, _, own, _ = first.shape
+    step = min(8, blocks)
+    whole = pl.BlockSpec((step, width, columns), lambda g: (g, 0, 0))
+    part = pl.BlockSpec((devices, step, own, width), lambda g: (0, g, 0, 0))
+    return pl.pallas_call(
+        finish_kernel,
+        out_shape=(jax.ShapeDtypeStruct(target.shape, jnp.float32),) * 2,
+        grid=(blocks // step,),
+        in_specs=[
+            whole,
+            pl.BlockSpec((step, width), lambda g: (g, 0)),
+            part,
+            part,
+            pl.BlockSpec(scales.shape, lambda g: (0, 0)),
+        ],
+        out_specs=(whole, whole),
+    )(target, diag, first, second, scales)
+
+
+def operate_kernel(slots, irow_ref, icol_ref, count_ref, blocks_ref, mine_ref, theirs_ref,
+                   image_ref, away_ref, sum_ref):
+    tile = pl.program_id(0)
+    own = mine_ref.shape[1]
+
+    @pl.when(tile == 0)
+    def _():
+        image_ref[...] = jnp.zeros_like(image_ref)
+        sum_ref[...] = jnp.zeros_like(sum_ref)
+
+    count = count_ref[tile]
+
+    def group(step, carry):
+        base = step * UNROLL
+        terms = []
+        for u in range(UNROLL):
+            k = base + u
+            i = irow_ref[tile * slots + k]
+            j = icol_ref[tile * slots + k]
+            block = blocks_ref[0, k]
+            at_i = jnp.concatenate([mine_ref[i], theirs_ref[i]], axis=0)
+            at_j = jnp.concatenate([mine_ref[j], theirs_ref[j]], axis=0)
+            direct = lax.dot_general(
+                at_j, block, (((1,), (1,)), ((), ())), preferred_element_type=jnp.float32
+            )
+            mirrored = lax.dot_general(
+                at_i, block, (((1,), (0,)), ((), ())), preferred_element_type=jnp.float32
+            )
+            terms.append((k < count, i, j, direct, mirrored))
+        for used, i, j, direct, mirrored in terms:
+            direct = jnp.where(used, direct, 0.0)
+            mirrored = jnp.where(used, mirrored, 0.0)
+            image_ref[i] += direct[:own]
+            sum_ref[i] += direct[own:]
+            image_ref[j] += mirrored[:own]
+            sum_ref[j] += mirrored[own:]
+        return carry
+
+    lax.fori_loop(0, (count + UNROLL - 1) // UNROLL, group, 0)
+
+    @pl.when(tile == pl.num_programs(0) - 1)
+    def _():
+        away_ref[...] = sum_ref[...].astype(away_ref.dtype)
+
+
+def operate(blocks, irow, icol, count, mine, theirs):
+    tiles, slots, width, _ = blocks.shape
+    whole = pl.BlockSpec(mine.shape, lambda t, *_: (0, 0, 0))
+    return pl.pallas_call(
+        functools.partial(operate_kernel, slots),
+        out_shape=(
+            jax.ShapeDtypeStruct(mine.shape, jnp.float32),
+            jax.ShapeDtypeStruct(mine.shape, jnp.bfloat16),
+        ),
+        grid_spec=pltpu.PrefetchScalarGridSpec(
+            num_scalar_prefetch=3,
+            grid=(tiles,),
+            in_specs=[
+                pl.BlockSpec((1, slots, width, width), lambda t, *_: (t, 0, 0, 0)),
+                whole,
+                whole,
+            ],
+            out_specs=(whole, whole),
+            scratch_shapes=[pltpu.VMEM(mine.shape, jnp.float32)],
+        ),
+        compiler_params=pltpu.CompilerParams(vmem_limit_bytes=40 * 2**20),
+        cost_estimate=pl.CostEstimate(
+            flops=tiles * slots * width**3 * 4, bytes_accessed=60 * 2**20, transcendentals=0
+        ),
+    )(irow, icol, count, blocks, mine, theirs)
+
+
+def by_columns(blocks, block_rows, block_cols, counts, diagonal, target):
+    grid = ("row", "col")
+    nrow, ncol = lax.axis_size("row"), lax.axis_size("col")
+    devices = nrow * ncol
+    stored = blocks[0, 0]
+    slots, width, _ = stored.shape
+    quarter = target.shape[0] // width
+    own = target.shape[1] // devices
+    row_blocks = ncol * quarter
+    half = slots // 2
+    row, col, core = lax.axis_index("row"), lax.axis_index("col"), lax.axis_index("rhs")
+
+    irow = row * row_blocks + block_rows[0, 0]
+    jcol = block_cols[0, 0]
+    icol = (jcol // quarter * ncol + col) * quarter + jcol % quarter
+
+    def every_other(index):
+        return jnp.where(core == 0, index[0::2], index[1::2])
+
+    used = (counts[0] - core + 1) // 2
+    names = jnp.concatenate([every_other(irow), every_other(icol), used])
+    names = jnp.pad(names, (0, -names.shape[0] % 1024)).reshape(-1, 128)
+    diag_own = diagonal.reshape(quarter, width)
+    target_blocks = target.reshape(quarter, width, target.shape[1])
+
+    tiles, field, all_names, all_diag = spread(
+        stored.reshape(half, 2, width, width), pack(target_blocks, devices), names, diag_own
+    )
+    all_names = all_names.reshape(devices, -1)
+    irows = all_names[:, :half].reshape(-1)
+    icols = all_names[:, half : 2 * half].reshape(-1)
+    used = all_names[:, 2 * half]
+    diag = all_diag.reshape(-1, 1, width)
+    swap = [(0, 1), (1, 0)]
+
+    def image_of(direction, low):
+        theirs = lax.ppermute(low, "rhs", swap)
+        here, away = operate(tiles, irows, icols, used, low, theirs)
+        return diag * direction + here + lax.ppermute(away, "rhs", swap).astype(jnp.float32)
+
+    def inner(a, b):
+        return jnp.sum(a * b, axis=(0, 2), keepdims=True)
+
+    def home(value):
+        parcel = value.astype(jnp.bfloat16).reshape(devices, quarter, own, width)
+        return lax.all_to_all(parcel, grid, split_axis=0, concat_axis=0, tiled=True)
+
+    low = field.reshape(-1, own, width)
+    start = low.astype(jnp.float32)
+    norm0 = inner(start, start)
+    image = image_of(start, low)
+    alpha1 = norm0 / inner(start, image)
+    first = start - alpha1 * image
+    norm1 = inner(first, first)
+    beta = norm1 / norm0
+    direction = first + beta * start
+    first_home = home(first)
+    image = image_of(direction, direction.astype(jnp.bfloat16))
+    alpha2 = norm1 / inner(direction, image)
+    second = first - alpha2 * image
+    second_home = home(second)
+    scales = jnp.stack([alpha1, alpha2, beta]).reshape(1, 3, own)
+    scales = lax.all_gather(scales, grid, axis=0, tiled=True)
+    scales = scales.transpose(1, 0, 2).reshape(3, devices * own)
+    answer, residual = finish(target_blocks, diag_own, first_home, second_home, scales)
+    return (answer.reshape(target.shape), residual.reshape(target.shape))
 
 
 def one_hot_slots(indices, valid, extent):
@@ -14,6 +330,15 @@
     highest = lax.Precision.HIGHEST
     nrow = lax.axis_size("row")
     ncol = lax.axis_size("col")
+    tile_bytes = blocks[0, 0].size * blocks.dtype.itemsize
+    if (
+        nrow * ncol * tile_bytes <= GATHER_BYTES
+        and ncol == 2
+        and lax.axis_size("rhs") == 2
+        and target.shape[1] == 16 * nrow * ncol
+        and blocks.shape[2] % (2 * UNROLL) == 0
+    ):
+        return by_columns(blocks, block_rows, block_cols, counts, diagonal, target)
     stored = blocks[0, 0]
     slots = stored.shape[0]
     width = stored.shape[1]

time: 976 us -> 386 us (0.40)
  waiting for transfers between devices: 689 us -> 14.9 us
  Pallas kernels: 0 us -> 226 us
  local copies, waits for them, and re-layouts: 83.1 us -> 6.4 us
  matrix products: 66.4 us -> 0 us
  blocking collectives: 52.6 us -> 116 us
  other arithmetic: 49.3 us -> 11 us
  between operations: 15.1 us -> 1.44 us
    all_gather x4 -> x0, waiting for transfers between devices: 589 us -> none  [the longest x2 475 us: on_device(): lax.all_gather(operate_field_low, 'row', axis=0, tiled=True)]
    pallas_call x0 -> x5, Pallas kernels: none -> 226 us  [the longest x1 176 us: spread(): pl.pallas_call(functools.partial(spread_kernel, nrow), out_shape=(jax.Sha...]
    reduce_scatter x2 -> x0, waiting for transfers between devices: 82.5 us -> none  [on_device(): lax.psum_scatter(direct_partial_value.reshape(row_blocks * width, ncols)....]
    dot_general x8 -> x0, matrix products: 66.4 us -> none  [the longest x2 26.2 us: on_device(): jnp.einsum('jk,kac->jac', cols_hot, tprod, precision=highest)]
    all_gather x0 -> x1, blocking collectives: none -> 64.5 us  [by_columns(): scales = lax.all_gather(scales, grid, axis=0, tiled=True)]
    psum x3 -> x0, blocking collectives: 52.6 us -> none  [the longest x2 34.8 us: squares(): return lax.psum(jnp.sum(vector * vector, axis=0), ('row', 'col'))]
    all_to_all x0 -> x1, blocking collectives: none -> 51.7 us  [home(): return lax.all_to_all(parcel, grid, split_axis=0, concat_axis=0, tiled=True)]
    convert_element_type x4 -> x0, local copies, waits for them, and re-layouts: 33.4 us -> none  [the longest x2 24 us: on_device(): parcel = partial_value.astype(jnp.bfloat16).reshape(nrow, local, ncols)]
  transfers between devices with their start and end apart: 8 -> 5, of which waited for: 8 -> 4; matrix products, arithmetic and copies ran while one was open for 17% -> 1% of each run, Pallas kernels for 0% -> 0%
where the time goes in v2:
time: 386 us; the launch traced here: 381 us
  Pallas kernels  226 us (59%)
  blocking collectives  116 us (30%)
  waiting for transfers between devices  14.9 us (4%)
  other arithmetic  11 us (3%)
  local copies, waits for them, and re-layouts  6.4 us (2%)
  starting transfers between devices  4.96 us (1%)
    pallas_call x1, Pallas kernels, spread(): pl.pallas_call(functools.partial(spread_kernel, nrow), out_shape=(jax.Sha...  176 us
    all_gather x1, blocking collectives, by_columns(): scales = lax.all_gather(scales, grid, axis=0, tiled=True)  64.5 us
    all_to_all x1, blocking collectives, home(): return lax.all_to_all(parcel, grid, split_axis=0, concat_axis=0, tiled=True)  51.7 us
    pallas_call x2, Pallas kernels, operate(): pl.pallas_call(functools.partial(operate_kernel, slots), out_shape=(jax.S...  33 us
    pallas_call x1, Pallas kernels, finish(): pl.pallas_call(finish_kernel, out_shape=(jax.ShapeDtypeStruct(target.shap...  10.1 us
  transfers between devices with their start and end apart: 5, of which 4 were waited for; matrix products, arithmetic and copies ran while one was open for 1% of the time, Pallas kernels for 0%

profile of v2, /device:TPU:12, one launch (start us, length us, event | category | flops | bytes accessed | tf_op | source)
XLA Modules:
  0.0 381.0 jit_solution(6017192838279575960)
XLA Ops:
  1.3 0.7 add_bitcast_fusion
  2.0 0.1 slice.21
  2.1 0.1 slice.22
  2.2 0.7 fusion.5
  2.9 0.1 slice.23
  3.0 0.1 slice.24
  3.2 0.1 pad_add_fusion
  3.3 0.6 pad_bitcast_fusion.names
  3.9 6.5 %shard_map.77.parcel = bf16[8,64,16,128]{3,2,1,0:T(8,128)(2,1)} custom-call(f32[64,128,128]{2,1,0:T(8,128)} %bitcast.50), custom_call_target="tpu_custom_call" | custom-call | tf_op jit(solution)/shard_map/pallas_call | solution.py:141
  10.4 176.4 %shard_map.78 = (bf16[8,48,128,128]{3,2,1,0:T(8,128)(2,1)}, bf16[8,64,16,128]{3,2,1,0:T(8,128)(2,1)}, s32[8,8,128]{2,1,0:T(8,128)}, f32[8,64,128]{2,1,0:T(8,128)}) custom-call(bf16[48,2,128,128]{3,2,1,0:T(8,128)(2,1)} %bitcast.57, bf16[8,64,16,128]{3,2,1,0:T(8,128)(2,1)} %shard_map.77.parcel, s32[8,128]{1,0:T(8,128)} %pad_bitcast_fusion.names, ...), custom_call_target="tpu_custom_call" | custom-call | tf_op jit(solution)/shard_map/pallas_call | solution.py:109
  186.8 0.1 collective-permute-start
  186.9 0.8 copy.21
  187.7 0.1 slice.30
  187.8 0.1 fusion.6
  187.8 0.1 reshape.110.irow_ref
  187.9 0.1 reshape.111.icol_ref
  188.0 0.1 copy.15
  188.1 3.2 collective-permute-done.theirs_ref
  191.3 0.0 copy-start
  191.3 1.6 copy-done
  192.9 0.0 copy-start.3
  192.9 16.5 %shard_map.79 = (f32[512,16,128]{2,1,0:T(8,128)S(1)}, bf16[512,16,128]{2,1,0:T(8,128)(2,1)S(1)}) custom-call(s32[384]{0:T(512)S(1)} %reshape.110.irow_ref, s32[384]{0:T(512)S(1)} %reshape.111.icol_ref, s32[8]{0:T(128)S(1)} %bitcast.48, bf16[8,48,128,128]{3,2,1,0:T(8,128)(2,1)} %get-tuple-element.15.blocks_ref, bf16[512,16,128]{2,1,0:T(8,128)(2,1)S(1)} %bitcast.47, ...), custom_call_target="tpu_custom_call" | custom-call | flops 3221225472 | bytes 62914560 | tf_op jit(solution)/shard_map/pallas_call | solution.py:233
  209.4 0.1 collective-permute-start.1
  209.5 0.7 multiply_reduce_fusion.2
  210.1 3.5 collective-permute-done.1
  213.6 0.0 copy-done.3
  213.6 1.4 fusion.2
  215.1 1.7 multiply_reduce_fusion.1
  216.8 0.7 fusion.4.mine_ref
  217.5 0.0 copy-start.1
  217.5 0.2 collective-permute-start.2
  217.7 4.0 %collective-permute-done.2.theirs_ref = bf16[512,16,128]{2,1,0:T(8,128)(2,1)S(1)} collective-permute-done((bf16[512,16,128]{2,1,0:T(8,128)(2,1)S(1)}, bf16[512,16,128]{2,1,0:T(8,128)(2,1)S(1)}, u32[]{:S(2)}, u32[]{:S(2)}) %collective-permute-start.2) | collective-permute-done | bytes 2097184 | tf_op jit(solution)/shard_map/ppermute | solution.py:293
  221.7 16.5 %shard_map.80 = (f32[512,16,128]{2,1,0:T(8,128)S(1)}, bf16[512,16,128]{2,1,0:T(8,128)(2,1)S(1)}) custom-call(s32[384]{0:T(512)S(1)} %reshape.110.irow_ref, s32[384]{0:T(512)S(1)} %reshape.111.icol_ref, s32[8]{0:T(128)S(1)} %bitcast.49, bf16[8,48,128,128]{3,2,1,0:T(8,128)(2,1)} %get-tuple-element.15.blocks_ref, bf16[512,16,128]{2,1,0:T(8,128)(2,1)S(1)} %fusion.4.mine_ref, ...), custom_call_target="tpu_custom_call" | custom-call | flops 3221225472 | bytes 62914560 | tf_op jit(solution)/shard_map/pallas_call | solution.py:233
  238.3 0.1 collective-permute-start.3
  238.3 4.1 %collective-permute-done.3 = bf16[512,16,128]{2,1,0:T(8,128)(2,1)S(1)} collective-permute-done((bf16[512,16,128]{2,1,0:T(8,128)(2,1)S(1)}, bf16[512,16,128]{2,1,0:T(8,128)(2,1)S(1)}, u32[]{:S(2)}, u32[]{:S(2)}) %collective-permute-start.3) | collective-permute-done | bytes 2097184 | tf_op jit(solution)/shard_map/ppermute | solution.py:295
  242.5 0.0 copy-done.1
  242.5 1.6 multiply_reduce_fusion
  244.1 2.8 subtract_convert_fusion
  246.9 51.7 %all_to_all.10.first_ref = bf16[8,64,16,128]{3,2,1,0:T(8,128)(2,1)} all-to-all(bf16[8,64,16,128]{3,2,1,0:T(8,128)(2,1)S(1)} %bitcast.52), channel_id=1, replica_groups=mesh['parts'=2,'row'=4,'col'=2,'rhs'=2] {'row','col'}, dimensions={0} | all-to-all | bytes 4194304 | tf_op jit(solution)/shard_map/all_to_all | solution.py:302
  298.6 4.5 %all-to-all-start.1 = ((bf16[8,64,16,128]{3,2,1,0:T(8,128)(2,1)}), bf16[8,64,16,128]{3,2,1,0:T(8,128)(2,1)S(1)}, u32[]{:S(2)}, u32[]{:S(2)}) async-start(bf16[8,64,16,128]{3,2,1,0:T(8,128)(2,1)} %bitcast.12), calls=%async_computation.1 | async-start | bytes 4194304 | tf_op jit(solution)/shard_map/all_to_all | solution.py:302
  303.2 64.5 %all-gather = f32[24,1,16,1]{2,3,1,0:T(1,128)S(1)} all-gather(f32[3,1,16,1]{2,3,1,0:T(1,128)S(1)} %pad_maximum_fusion), channel_id=2, replica_groups=mesh['parts'=2,'row'=4,'col'=2,'rhs'=2] {'row','col'}, dimensions={0}, use_global_device_ids=true | all-gather | bytes 1728 | tf_op jit(solution)/shard_map/all_gather | solution.py:319
  367.6 0.5 broadcast.24
  368.2 0.7 reduce.4
  368.9 0.7 reshape.115.scale_ref
  369.5 0.0 all-to-all-done.1.second_ref
  369.5 0.0 copy-start.2
  369.5 1.3 copy-done.2
  370.8 10.1 %shard_map.81 = (f32[64,128,128]{2,1,0:T(8,128)}, f32[64,128,128]{2,1,0:T(8,128)}) custom-call(f32[64,128,128]{2,1,0:T(8,128)} %bitcast.51, f32[64,128]{1,0:T(8,128)} %bitcast.59, bf16[8,64,16,128]{3,2,1,0:T(8,128)(2,1)} %all_to_all.10.first_ref, bf16[8,64,16,128]{3,2,1,0:T(8,128)(2,1)} %copy-done.2, f32[3,128]{1,0:T(4,128)} %reshape.115.scale_ref), custom_call_target="tpu_custom_call" | custom-call | tf_op jit(solution)/shard_map/pallas_call | solution.py:170
  (7 shorter events, 0.0 us)
Async XLA Ops:
  186.8 4.4 %collective-permute-start = (bf16[512,16,128]{2,1,0:T(8,128)(2,1)}, bf16[512,16,128]{2,1,0:T(8,128)(2,1)S(1)}, u32[]{:S(2)}, u32[]{:S(2)}) collective-permute-start(bf16[512,16,128]{2,1,0:T(8,128)(2,1)} %bitcast.46), channel_id=1, source_target_pairs={{0,1},{1,0},{2,3},{3,2},{4,5},{5,4},{6,7},{7,6},{8,9},{9,8},{10,11... | collective-permute-start | bytes 6291464 | tf_op jit(solution)/shard_map/ppermute | solution.py:293
  191.3 1.6 copy-start
  192.9 20.8 %copy-start.3 = (f32[8,64,128]{2,1,0:T(8,128)S(1)}, f32[8,64,128]{2,1,0:T(8,128)}, u32[]{:S(2)}) copy-start(f32[8,64,128]{2,1,0:T(8,128)} %get-tuple-element.13) | copy-start | bytes 786436
  209.4 4.2 %collective-permute-start.1 = (bf16[512,16,128]{2,1,0:T(8,128)(2,1)S(1)}, bf16[512,16,128]{2,1,0:T(8,128)(2,1)S(1)}, u32[]{:S(2)}, u32[]{:S(2)}) collective-permute-start(bf16[512,16,128]{2,1,0:T(8,128)(2,1)S(1)} %get-tuple-element.17), channel_id=1, source_target_pairs={{0,1},{1,0},{2,3},{3,2},{4,5},{5,4},{6,7},{7,6},{8,9},{9,8},{10,11... | collective-permute-start | bytes 6291464 | tf_op jit(solution)/shard_map/ppermute | solution.py:295
  217.5 25.0 %copy-start.1 = (bf16[8,64,16,128]{3,2,1,0:T(8,128)(2,1)S(1)}, bf16[8,64,16,128]{3,2,1,0:T(8,128)(2,1)}, u32[]{:S(2)}) copy-start(bf16[8,64,16,128]{3,2,1,0:T(8,128)(2,1)} %get-tuple-element.12) | copy-start | bytes 6291460
  217.5 4.2 %collective-permute-start.2 = (bf16[512,16,128]{2,1,0:T(8,128)(2,1)S(1)}, bf16[512,16,128]{2,1,0:T(8,128)(2,1)S(1)}, u32[]{:S(2)}, u32[]{:S(2)}) collective-permute-start(bf16[512,16,128]{2,1,0:T(8,128)(2,1)S(1)} %fusion.4.mine_ref), channel_id=1, source_target_pairs={{0,1},{1,0},{2,3},{3,2},{4,5},{5,4},{6,7},{7,6},{8,9},{9,8},{10,11... | collective-permute-start | bytes 6291464 | tf_op jit(solution)/shard_map/ppermute | solution.py:293
  238.3 4.2 %collective-permute-start.3 = (bf16[512,16,128]{2,1,0:T(8,128)(2,1)S(1)}, bf16[512,16,128]{2,1,0:T(8,128)(2,1)S(1)}, u32[]{:S(2)}, u32[]{:S(2)}) collective-permute-start(bf16[512,16,128]{2,1,0:T(8,128)(2,1)S(1)} %get-tuple-element.19), channel_id=1, source_target_pairs={{0,1},{1,0},{2,3},{3,2},{4,5},{5,4},{6,7},{7,6},{8,9},{9,8},{10,11... | collective-permute-start | bytes 6291464 | tf_op jit(solution)/shard_map/ppermute | solution.py:295
  298.6 70.9 %all-to-all-start.1 = ((bf16[8,64,16,128]{3,2,1,0:T(8,128)(2,1)}), bf16[8,64,16,128]{3,2,1,0:T(8,128)(2,1)S(1)}, u32[]{:S(2)}, u32[]{:S(2)}) async-start(bf16[8,64,16,128]{3,2,1,0:T(8,128)(2,1)} %bitcast.12), calls=%async_computation.1 | async-start | bytes 4194304 | tf_op jit(solution)/shard_map/all_to_all | solution.py:302
  369.5 1.3 copy-start.2

commit v3 on v2

--- a/solution.py
+++ b/solution.py
@@ -38,30 +38,32 @@
     pl.semaphore_wait(barrier, devices - 1)
 
     half = tiles.shape[1]
-    quart = half // 2
+    lanes = ring_send.shape[0]
+    piece = half // lanes
     hops = []
 
-    def hop(way, step):
+    def hop(lane, step):
+        way = lane % 2
         r, c = device_at(place + (1 if way == 0 else -1))
         if step == 0:
-            source = stored.at[pl.ds(way * quart, quart), core]
+            source = stored.at[pl.ds(lane * piece, piece), core]
             origin = me
         else:
             orow, ocol = device_at(place + (-step if way == 0 else step))
             origin = orow * 2 + ocol
-            source = tiles.at[origin, pl.ds(way * quart, quart)]
+            source = tiles.at[origin, pl.ds(lane * piece, piece)]
         copy = pltpu.make_async_remote_copy(
             src_ref=source,
-            dst_ref=tiles.at[origin, pl.ds(way * quart, quart)],
-            send_sem=ring_send.at[way, step],
-            recv_sem=ring_recv.at[way, step],
+            dst_ref=tiles.at[origin, pl.ds(lane * piece, piece)],
+            send_sem=ring_send.at[lane, step],
+            recv_sem=ring_recv.at[lane, step],
             device_id={"row": r, "col": c},
             device_id_type=MESH,
         )
         copy.start()
         return copy
 
-    now = [hop(0, 0), hop(1, 0)]
+    now = [hop(lane, 0) for lane in range(lanes)]
     straight = []
     pairs = ((names, all_names, False), (diag, all_diag, False), (parcel, field, True))
     for n, (source, target, apart) in enumerate(pairs):
@@ -88,11 +90,11 @@
         copy.start()
         local.append(copy)
     for step in range(1, devices):
-        for way in range(2):
-            now[way].wait_recv()
+        for lane in range(lanes):
+            now[lane].wait_recv()
             if step < devices - 1:
-                hops.append(now[way])
-                now[way] = hop(way, step)
+                hops.append(now[lane])
+                now[lane] = hop(lane, step)
     hops += now
     for copy in hops:
         copy.wait_send()
@@ -106,6 +108,7 @@
     nrow = lax.axis_size("row")
     devices = 2 * nrow
     half, cores, width, _ = stored.shape
+    lanes = 6 if half % 6 == 0 else 2
     return pl.pallas_call(
         functools.partial(spread_kernel, nrow),
         out_shape=(
@@ -117,14 +120,75 @@
         in_specs=[ANY] * 4,
         out_specs=[ANY] * 4,
         scratch_shapes=[
-            pltpu.SemaphoreType.DMA((2, devices - 1)),
-            pltpu.SemaphoreType.DMA((2, devices - 1)),
+            pltpu.SemaphoreType.DMA((lanes, devices - 1)),
+            pltpu.SemaphoreType.DMA((lanes, devices - 1)),
             pltpu.SemaphoreType.DMA((3, devices - 1)),
             pltpu.SemaphoreType.DMA((3, devices - 1)),
             pltpu.SemaphoreType.DMA((4,)),
         ],
         compiler_params=pltpu.CompilerParams(collective_id=0, has_side_effects=True),
     )(stored, parcel, names, diag)
+
+
+def home_kernel(nrow, early, first, parcel, scale, late, field, scales, send, recv, own_sem):
+    devices = 2 * nrow
+    me = lax.axis_index("row") * 2 + lax.axis_index("col")
+
+    def peer(offset):
+        other = lax.rem(me + offset, devices)
+        return {"row": other // 2, "col": lax.rem(other, 2)}
+
+    barrier = pltpu.get_barrier_semaphore()
+    for offset in range(1, devices):
+        pl.semaphore_signal(barrier, inc=1, device_id=peer(offset), device_id_type=MESH)
+    pl.semaphore_wait(barrier, devices - 1)
+    copies = []
+    rest = pl.ds(early, late.shape[1])
+    for n, target in enumerate((scales, late, field)):
+        for offset in range(1, devices):
+            to = lax.rem(me + offset, devices)
+            copy = pltpu.make_async_remote_copy(
+                src_ref=(scale, first.at[to, rest], parcel.at[to])[n],
+                dst_ref=target.at[me],
+                send_sem=send.at[n, offset - 1],
+                recv_sem=recv.at[n, offset - 1],
+                device_id=peer(offset),
+                device_id_type=MESH,
+            )
+            copy.start()
+            copies.append(copy)
+    owns = (
+        (scale, scales.at[me]),
+        (first.at[me, rest], late.at[me]),
+        (parcel.at[me], field.at[me]),
+    )
+    for n, (source, target) in enumerate(owns):
+        copy = pltpu.make_async_copy(source, target, own_sem.at[n])
+        copy.start()
+        copies.append(copy)
+    for copy in copies:
+        copy.wait()
+
+
+def send_home(first, parcel, scale, early):
+    nrow = lax.axis_size("row")
+    devices, blocks = parcel.shape[:2]
+    return pl.pallas_call(
+        functools.partial(home_kernel, nrow, early),
+        out_shape=(
+            jax.ShapeDtypeStruct((devices, blocks - early) + parcel.shape[2:], parcel.dtype),
+            jax.ShapeDtypeStruct(parcel.shape, parcel.dtype),
+            jax.ShapeDtypeStruct((devices,) + scale.shape, scale.dtype),
+        ),
+        in_specs=[ANY] * 3,
+        out_specs=[ANY] * 3,
+        scratch_shapes=[
+            pltpu.SemaphoreType.DMA((3, devices - 1)),
+            pltpu.SemaphoreType.DMA((3, devices - 1)),
+            pltpu.SemaphoreType.DMA((3,)),
+        ],
+        compiler_params=pltpu.CompilerParams(collective_id=1, has_side_effects=True),
+    )(first, parcel, scale)
 
 
 def pack_kernel(target_ref, parcel_ref):
@@ -147,9 +211,22 @@
     )(target)
 
 
-def finish_kernel(target_ref, diag_ref, first_ref, second_ref, scale_ref, answer_ref, residual_ref):
+def finish_kernel(me_ref, target_ref, diag_ref, early_ref, late_ref, second_ref, scale_ref,
+                  answer_ref, residual_ref, first_ref):
     blocks, width, columns = target_ref.shape
     alpha1, alpha2, beta = scale_ref[0:1], scale_ref[1:2], scale_ref[2:3]
+    devices = second_ref.shape[0]
+    late = pl.program_id(0) >= pl.num_programs(0) // 2
+
+    @pl.when(late)
+    def _():
+        first_ref[...] = late_ref[...]
+
+    @pl.when(jnp.logical_not(late))
+    def _():
+        for source in range(devices):
+            first_ref[source] = early_ref[lax.rem(me_ref[0] - source + devices, devices)]
+
     for b in range(blocks):
         target = target_ref[b]
         diag = jnp.transpose(jnp.broadcast_to(diag_ref[pl.ds(b, 1), :], (columns, width)))
@@ -161,10 +238,11 @@
         residual_ref[b] = second + lost1 - alpha2 * diag * (lost1 + beta * lost)
 
 
-def finish(target, diag, first, second, scales):
+def finish(me, target, diag, early, late, second, scales):
     blocks, width, columns = target.shape
-    devices, _, own, _ = first.shape
-    step = min(8, blocks)
+    devices, _, own, _ = second.shape
+    step = min(8, blocks // 2)
+    last = blocks // step // 2
     whole = pl.BlockSpec((step, width, columns), lambda g: (g, 0, 0))
     part = pl.BlockSpec((devices, step, own, width), lambda g: (0, g, 0, 0))
     return pl.pallas_call(
@@ -172,14 +250,17 @@
         out_shape=(jax.ShapeDtypeStruct(target.shape, jnp.float32),) * 2,
         grid=(blocks // step,),
         in_specs=[
+            pl.BlockSpec(memory_space=pltpu.SMEM),
             whole,
             pl.BlockSpec((step, width), lambda g: (g, 0)),
-            part,
+            pl.BlockSpec((devices, step, own, width), lambda g: (0, jnp.minimum(g, last - 1), 0, 0)),
+            pl.BlockSpec((devices, step, own, width), lambda g: (0, jnp.maximum(g - last, 0), 0, 0)),
             part,
             pl.BlockSpec(scales.shape, lambda g: (0, 0)),
         ],
         out_specs=(whole, whole),
-    )(target, diag, first, second, scales)
+        scratch_shapes=[pltpu.VMEM((devices, step, own, width), jnp.bfloat16)],
+    )(me, target, diag, early, late, second, scales)
 
 
 def operate_kernel(slots, irow_ref, icol_ref, count_ref, blocks_ref, mine_ref, theirs_ref,
@@ -289,36 +370,55 @@
     diag = all_diag.reshape(-1, 1, width)
     swap = [(0, 1), (1, 0)]
 
-    def image_of(direction, low):
+    def image_of(direction, low, beside=()):
         theirs = lax.ppermute(low, "rhs", swap)
         here, away = operate(tiles, irows, icols, used, low, theirs)
-        return diag * direction + here + lax.ppermute(away, "rhs", swap).astype(jnp.float32)
+        (here, away), beside = lax.optimization_barrier(((here, away), beside))
+        away = lax.ppermute(away, "rhs", swap).astype(jnp.float32)
+        return diag * direction + here + away, beside
 
     def inner(a, b):
         return jnp.sum(a * b, axis=(0, 2), keepdims=True)
 
-    def home(value):
-        parcel = value.astype(jnp.bfloat16).reshape(devices, quarter, own, width)
-        return lax.all_to_all(parcel, grid, split_axis=0, concat_axis=0, tiled=True)
+    me = row * ncol + col
+
+    def parcels(value):
+        return value.astype(jnp.bfloat16).reshape(devices, quarter, own, width)
+
+    def home_by_offset(parcel):
+        pieces = []
+        for offset in range(devices):
+            piece = lax.dynamic_index_in_dim(parcel, (me + offset) % devices, 0, keepdims=False)
+            if offset:
+                pairs = [(d, (d + offset) % devices) for d in range(devices)]
+                piece = lax.ppermute(piece, grid, pairs)
+            pieces.append(piece)
+        return pieces
 
     low = field.reshape(-1, own, width)
     start = low.astype(jnp.float32)
     norm0 = inner(start, start)
-    image = image_of(start, low)
+    image, _ = image_of(start, low)
     alpha1 = norm0 / inner(start, image)
     first = start - alpha1 * image
     norm1 = inner(first, first)
     beta = norm1 / norm0
     direction = first + beta * start
-    first_home = home(first)
-    image = image_of(direction, direction.astype(jnp.bfloat16))
+    first_parcel = parcels(first)
+    early = quarter // 2
+    pieces = home_by_offset(first_parcel[:, :early])
+    image, pieces = image_of(direction, direction.astype(jnp.bfloat16), pieces)
+    first_early = jnp.stack(pieces)
     alpha2 = norm1 / inner(direction, image)
     second = first - alpha2 * image
-    second_home = home(second)
-    scales = jnp.stack([alpha1, alpha2, beta]).reshape(1, 3, own)
-    scales = lax.all_gather(scales, grid, axis=0, tiled=True)
+    scale = jnp.stack([alpha1, alpha2, beta]).reshape(3, own)
+    scale = jnp.pad(scale, ((0, 5), (0, 128 - own)))
+    first_late, second_home, scales = send_home(first_parcel, parcels(second), scale, early)
+    scales = scales[:, :3, :own]
     scales = scales.transpose(1, 0, 2).reshape(3, devices * own)
-    answer, residual = finish(target_blocks, diag_own, first_home, second_home, scales)
+    answer, residual = finish(
+        me.reshape(1), target_blocks, diag_own, first_early, first_late, second_home, scales
+    )
     return (answer.reshape(target.shape), residual.reshape(target.shape))
 
 
@@ -337,6 +437,7 @@
         and lax.axis_size("rhs") == 2
         and target.shape[1] == 16 * nrow * ncol
         and blocks.shape[2] % (2 * UNROLL) == 0
+        and target.shape[0] // blocks.shape[3] % 16 == 0
     ):
         return by_columns(blocks, block_rows, block_cols, counts, diagonal, target)
     stored = blocks[0, 0]

time: 386 us -> 361 us (0.935)
  blocking collectives: 116 us -> 0 us
  Pallas kernels: 226 us -> 310 us
  starting transfers between devices: 4.96 us -> 12.7 us
  waiting for transfers between devices: 14.9 us -> 10.9 us
    pallas_call x0 -> x1, Pallas kernels: none -> 82.8 us  [send_home(): pl.pallas_call(functools.partial(home_kernel, nrow, early), out_shape=(ja...]
    all_gather x1 -> x0, blocking collectives: 64.5 us -> none  [by_columns(): scales = lax.all_gather(scales, grid, axis=0, tiled=True)]
    all_to_all x1 -> x0, blocking collectives: 51.7 us -> none  [home(): return lax.all_to_all(parcel, grid, split_axis=0, concat_axis=0, tiled=True)]
    ppermute x2 -> x9, starting transfers between devices: 0.14 us -> 12.5 us  [the longest x7 12.3 us: home_by_offset(): piece = lax.ppermute(piece, grid, pairs)]
    all_to_all x1 -> x0, starting transfers between devices: 4.55 us -> none  [home(): return lax.all_to_all(parcel, grid, split_axis=0, concat_axis=0, tiled=True)]
    convert_element_type x2 -> x3, other arithmetic: 3.53 us -> 7.7 us  [the longest x2 5.66 us: parcels(): return value.astype(jnp.bfloat16).reshape(devices, quarter, own, width)]
    ppermute x2, waiting for transfers between devices: 7.23 us -> 3.21 us  [image_of(): theirs = lax.ppermute(low, 'rhs', swap)]
  transfers between devices with their start and end apart: 5 -> 11, of which waited for: 4 -> 4; matrix products, arithmetic and copies ran while one was open for 1% -> 1% of each run, Pallas kernels for 0% -> 5%
where the time goes in v3:
time: 361 us; the launch traced here: 357 us
  Pallas kernels  310 us (86%)
  other arithmetic  13.6 us (4%)
  starting transfers between devices  12.7 us (4%)
  waiting for transfers between devices  10.9 us (3%)
  local copies, waits for them, and re-layouts  7.82 us (2%)
    pallas_call x1, Pallas kernels, spread(): pl.pallas_call(functools.partial(spread_kernel, nrow), out_shape=(jax.Sha...  175 us
    pallas_call x1, Pallas kernels, send_home(): pl.pallas_call(functools.partial(home_kernel, nrow, early), out_shape=(ja...  82.8 us
    pallas_call x2, Pallas kernels, operate(): pl.pallas_call(functools.partial(operate_kernel, slots), out_shape=(jax.S...  35.3 us
    ppermute x7, starting transfers between devices, home_by_offset(): piece = lax.ppermute(piece, grid, pairs)  12.3 us
    pallas_call x1, Pallas kernels, finish(): pl.pallas_call(finish_kernel, out_shape=(jax.ShapeDtypeStruct(target.shap...  10.2 us
    ppermute x2, waiting for transfers between devices, image_of(): away = lax.ppermute(away, 'rhs', swap).astype(jnp.float32)  7.29 us
  transfers between devices with their start and end apart: 11, of which 4 were waited for; matrix products, arithmetic and copies ran while one was open for 1% of the time, Pallas kernels for 5%

profile of v3, /device:TPU:12, one launch (start us, length us, event | category | flops | bytes accessed | tf_op | source)
XLA Modules:
  0.0 356.8 jit_solution(13114713910326718200)
XLA Ops:
  1.3 0.7 fusion.5
  2.0 0.1 slice.29
  2.1 0.1 slice.30
  2.2 0.7 add_bitcast_fusion
  2.9 0.1 slice.27
  3.0 0.1 slice.28
  3.2 6.5 %shard_map.77.parcel = bf16[8,64,16,128]{3,2,1,0:T(8,128)(2,1)} custom-call(f32[64,128,128]{2,1,0:T(8,128)} %bitcast.85), custom_call_target="tpu_custom_call" | custom-call | tf_op jit(solution)/shard_map/pallas_call | solution.py:205
  9.7 0.1 pad_add_fusion
  9.8 0.6 pad_bitcast_fusion.names
  10.4 175.4 %shard_map.78 = (bf16[8,48,128,128]{3,2,1,0:T(8,128)(2,1)}, bf16[8,64,16,128]{3,2,1,0:T(8,128)(2,1)}, s32[8,8,128]{2,1,0:T(8,128)}, f32[8,64,128]{2,1,0:T(8,128)}) custom-call(bf16[48,2,128,128]{3,2,1,0:T(8,128)(2,1)} %bitcast.94, bf16[8,64,16,128]{3,2,1,0:T(8,128)(2,1)} %shard_map.77.parcel, s32[8,128]{1,0:T(8,128)} %pad_bitcast_fusion.names, ...), custom_call_target="tpu_custom_call" | custom-call | tf_op jit(solution)/shard_map/pallas_call | solution.py:112
  185.8 0.1 collective-permute-start
  185.8 0.8 copy.15
  186.6 0.1 slice.38
  186.7 0.1 fusion.7
  186.8 0.1 reshape.113.irow_ref
  186.8 0.1 reshape.114.icol_ref
  186.9 0.1 copy.11
  187.0 3.2 collective-permute-done.theirs_ref
  190.2 1.6 copy-done
  191.8 16.9 %shard_map.79 = (f32[512,16,128]{2,1,0:T(8,128)S(1)}, bf16[512,16,128]{2,1,0:T(8,128)(2,1)S(1)}) custom-call(s32[384]{0:T(512)S(1)} %reshape.113.irow_ref, s32[384]{0:T(512)S(1)} %reshape.114.icol_ref, s32[8]{0:T(128)S(1)} %bitcast.83, bf16[8,48,128,128]{3,2,1,0:T(8,128)(2,1)} %get-tuple-element.26.blocks_ref, bf16[512,16,128]{2,1,0:T(8,128)(2,1)S(1)} %bitcast.82, ...), custom_call_target="tpu_custom_call" | custom-call | flops 3221225472 | bytes 62914560 | tf_op jit(solution)/shard_map/pallas_call | solution.py:314
  208.7 0.2 collective-permute-start.1
  208.9 0.7 multiply_reduce_fusion.2
  209.5 3.4 collective-permute-done.1
  212.9 1.4 fusion.2
  214.3 0.1 copy-done.1
  214.5 2.7 fusion.6
  217.2 0.7 multiply_reduce_fusion.1
  217.8 2.0 fusion.4.mine_ref
  219.9 0.1 collective-permute-start.2
  220.0 1.4 slice.39
  221.4 0.2 dynamic-slice_bitcast_fusion
  221.6 0.6 collective-permute-start.3
  222.2 1.5 collective-permute-start.4
  223.7 4.8 %collective-permute-start.6 = (bf16[32,16,128]{2,1,0:T(8,128)(2,1)S(1)}, bf16[32,16,128]{2,1,0:T(8,128)(2,1)S(1)}, u32[]{:S(2)}, u32[]{:S(2)}) collective-permute-start(bf16[32,16,128]{2,1,0:T(8,128)(2,1)S(1)} %get-tuple-element.53), channel_id=1, source_target_pairs={{0,8},{2,10},{4,12},{6,14},{8,0},{10,2},{12,4},{14,6},{1,9},{3,11}... | collective-permute-start | bytes 393224 | tf_op jit(solution)/shard_map/ppermute | solution.py:394
  228.5 0.4 collective-permute-done.3
  228.9 1.5 collective-permute-start.8
  230.4 0.0 collective-permute-done.2.theirs_ref
  230.4 3.9 %collective-permute-start.9 = (bf16[32,16,128]{2,1,0:T(8,128)(2,1)S(1)}, bf16[32,16,128]{2,1,0:T(8,128)(2,1)S(1)}, u32[]{:S(2)}, u32[]{:S(2)}) collective-permute-start(bf16[32,16,128]{2,1,0:T(8,128)(2,1)S(1)} %get-tuple-element.50), channel_id=1, source_target_pairs={{0,14},{2,0},{4,2},{6,4},{8,6},{10,8},{12,10},{14,12},{1,15},{3,1}... | collective-permute-start | bytes 393224 | tf_op jit(solution)/shard_map/ppermute | solution.py:394
  234.3 18.5 %shard_map.80 = (f32[512,16,128]{2,1,0:T(8,128)S(1)}, bf16[512,16,128]{2,1,0:T(8,128)(2,1)S(1)}) custom-call(s32[384]{0:T(512)S(1)} %reshape.113.irow_ref, s32[384]{0:T(512)S(1)} %reshape.114.icol_ref, s32[8]{0:T(128)S(1)} %bitcast.84, bf16[8,48,128,128]{3,2,1,0:T(8,128)(2,1)} %get-tuple-element.26.blocks_ref, bf16[512,16,128]{2,1,0:T(8,128)(2,1)} %fusion.4.mine_ref, ...), custom_call_target="tpu_custom_call" | custom-call | flops 3221225472 | bytes 62914560 | tf_op jit(solution)/shard_map/pallas_call | solution.py:314
  252.8 0.1 collective-permute-start.10
  253.1 3.9 %collective-permute-done.10 = bf16[512,16,128]{2,1,0:T(8,128)(2,1)S(1)} collective-permute-done((bf16[512,16,128]{2,1,0:T(8,128)(2,1)S(1)}, bf16[512,16,128]{2,1,0:T(8,128)(2,1)S(1)}, u32[]{:S(2)}, u32[]{:S(2)}) %collective-permute-start.10) | collective-permute-done | bytes 2097184 | tf_op jit(solution)/shard_map/ppermute | solution.py:377
  257.0 1.7 multiply_reduce_fusion
  258.8 0.6 pad.9.scale
  259.4 3.0 subtract_convert_fusion
  262.4 82.8 %shard_map.81 = (bf16[8,32,16,128]{3,2,1,0:T(8,128)(2,1)}, bf16[8,64,16,128]{3,2,1,0:T(8,128)(2,1)}, f32[8,8,128]{2,1,0:T(8,128)}) custom-call(bf16[8,64,16,128]{3,2,1,0:T(8,128)(2,1)} %bitcast.88, bf16[8,64,16,128]{3,2,1,0:T(8,128)(2,1)} %bitcast.89, f32[8,128]{1,0:T(8,128)} %pad.9.scale), custom_call_target="tpu_custom_call" | custom-call | tf_op jit(solution)/shard_map/pallas_call | solution.py:176
  345.2 0.8 slice_bitcast_fusion
  345.9 0.7 reshape.119.scale_ref
  346.6 10.2 %shard_map.82 = (f32[64,128,128]{2,1,0:T(8,128)}, f32[64,128,128]{2,1,0:T(8,128)}) custom-call(s32[1]{0:T(128)} %bitcast.me_ref, f32[64,128,128]{2,1,0:T(8,128)} %bitcast.86, f32[64,128]{1,0:T(8,128)} %bitcast.96, bf16[8,32,16,128]{3,2,1,0:T(8,128)(2,1)} %copy-done.5, bf16[8,32,16,128]{3,2,1,0:T(8,128)(2,1)} %get-tuple-element.43.late_ref, ...), custom_call_target="tpu_custom_call" | custom-call | tf_op jit(solution)/shard_map/pallas_call | solution.py:248
  (33 shorter events, 0.2 us)
Async XLA Ops:
  185.8 4.4 %collective-permute-start = (bf16[512,16,128]{2,1,0:T(8,128)(2,1)}, bf16[512,16,128]{2,1,0:T(8,128)(2,1)S(1)}, u32[]{:S(2)}, u32[]{:S(2)}) collective-permute-start(bf16[512,16,128]{2,1,0:T(8,128)(2,1)} %bitcast.81), channel_id=1, source_target_pairs={{0,1},{1,0},{2,3},{3,2},{4,5},{5,4},{6,7},{7,6},{8,9},{9,8},{10,11... | collective-permute-start | bytes 6291464 | tf_op jit(solution)/shard_map/ppermute | solution.py:374
  190.2 1.6 copy-start
  191.8 21.1 %copy-start.4 = (f32[8,64,128]{2,1,0:T(8,128)S(1)}, f32[8,64,128]{2,1,0:T(8,128)}, u32[]{:S(2)}) copy-start(f32[8,64,128]{2,1,0:T(8,128)} %get-tuple-element.28) | copy-start | bytes 786436
  208.7 4.2 %collective-permute-start.1 = (bf16[512,16,128]{2,1,0:T(8,128)(2,1)S(1)}, bf16[512,16,128]{2,1,0:T(8,128)(2,1)S(1)}, u32[]{:S(2)}, u32[]{:S(2)}) collective-permute-start(bf16[512,16,128]{2,1,0:T(8,128)(2,1)S(1)} %get-tuple-element.30), channel_id=1, source_target_pairs={{0,1},{1,0},{2,3},{3,2},{4,5},{5,4},{6,7},{7,6},{8,9},{9,8},{10,11... | collective-permute-start | bytes 6291464 | tf_op jit(solution)/shard_map/ppermute | solution.py:377
  212.9 1.6 copy-start.1
  217.2 2.7 copy-start.2
  219.9 10.5 %collective-permute-start.2 = (bf16[512,16,128]{2,1,0:T(8,128)(2,1)}, bf16[512,16,128]{2,1,0:T(8,128)(2,1)}, u32[]{:S(2)}, u32[]{:S(2)}) collective-permute-start(bf16[512,16,128]{2,1,0:T(8,128)(2,1)} %fusion.4.mine_ref), channel_id=1, source_target_pairs={{0,1},{1,0},{2,3},{3,2},{4,5},{5,4},{6,7},{7,6},{8,9},{9,8},{10,11... | collective-permute-start | bytes 6291464 | tf_op jit(solution)/shard_map/ppermute | solution.py:374
  221.6 7.3 %collective-permute-start.3 = (bf16[32,16,128]{2,1,0:T(8,128)(2,1)S(1)}, bf16[32,16,128]{2,1,0:T(8,128)(2,1)S(1)}, u32[]{:S(2)}, u32[]{:S(2)}) collective-permute-start(bf16[32,16,128]{2,1,0:T(8,128)(2,1)S(1)} %get-tuple-element.56), channel_id=1, source_target_pairs={{0,2},{2,4},{4,6},{6,8},{8,10},{10,12},{12,14},{14,0},{1,3},{3,5},... | collective-permute-start | bytes 393224 | tf_op jit(solution)/shard_map/ppermute | solution.py:394
  222.2 6.7 %collective-permute-start.4 = (bf16[32,16,128]{2,1,0:T(8,128)(2,1)S(1)}, bf16[32,16,128]{2,1,0:T(8,128)(2,1)S(1)}, u32[]{:S(2)}, u32[]{:S(2)}) collective-permute-start(bf16[32,16,128]{2,1,0:T(8,128)(2,1)S(1)} %get-tuple-element.55), channel_id=1, source_target_pairs={{0,4},{2,6},{4,8},{6,10},{8,12},{10,14},{12,0},{14,2},{1,5},{3,7},... | collective-permute-start | bytes 393224 | tf_op jit(solution)/shard_map/ppermute | solution.py:394
  223.7 29.0 %collective-permute-start.5 = (bf16[32,16,128]{2,1,0:T(8,128)(2,1)S(1)}, bf16[32,16,128]{2,1,0:T(8,128)(2,1)S(1)}, u32[]{:S(2)}, u32[]{:S(2)}) collective-permute-start(bf16[32,16,128]{2,1,0:T(8,128)(2,1)S(1)} %get-tuple-element.54), channel_id=1, source_target_pairs={{0,6},{2,8},{4,10},{6,12},{8,14},{10,0},{12,2},{14,4},{1,7},{3,9},... | collective-permute-start | bytes 393224 | tf_op jit(solution)/shard_map/ppermute | solution.py:394
  223.7 29.1 %collective-permute-start.6 = (bf16[32,16,128]{2,1,0:T(8,128)(2,1)S(1)}, bf16[32,16,128]{2,1,0:T(8,128)(2,1)S(1)}, u32[]{:S(2)}, u32[]{:S(2)}) collective-permute-start(bf16[32,16,128]{2,1,0:T(8,128)(2,1)S(1)} %get-tuple-element.53), channel_id=1, source_target_pairs={{0,8},{2,10},{4,12},{6,14},{8,0},{10,2},{12,4},{14,6},{1,9},{3,11}... | collective-permute-start | bytes 393224 | tf_op jit(solution)/shard_map/ppermute | solution.py:394
  228.9 23.9 %collective-permute-start.7 = (bf16[32,16,128]{2,1,0:T(8,128)(2,1)S(1)}, bf16[32,16,128]{2,1,0:T(8,128)(2,1)S(1)}, u32[]{:S(2)}, u32[]{:S(2)}) collective-permute-start(bf16[32,16,128]{2,1,0:T(8,128)(2,1)S(1)} %get-tuple-element.52), channel_id=1, source_target_pairs={{0,10},{2,12},{4,14},{6,0},{8,2},{10,4},{12,6},{14,8},{1,11},{3,13... | collective-permute-start | bytes 393224 | tf_op jit(solution)/shard_map/ppermute | solution.py:394
  228.9 23.9 %collective-permute-start.8 = (bf16[32,16,128]{2,1,0:T(8,128)(2,1)S(1)}, bf16[32,16,128]{2,1,0:T(8,128)(2,1)S(1)}, u32[]{:S(2)}, u32[]{:S(2)}) collective-permute-start(bf16[32,16,128]{2,1,0:T(8,128)(2,1)S(1)} %get-tuple-element.51), channel_id=1, source_target_pairs={{0,12},{2,14},{4,0},{6,2},{8,4},{10,6},{12,8},{14,10},{1,13},{3,15... | collective-permute-start | bytes 393224 | tf_op jit(solution)/shard_map/ppermute | solution.py:394
  230.4 22.4 %collective-permute-start.9 = (bf16[32,16,128]{2,1,0:T(8,128)(2,1)S(1)}, bf16[32,16,128]{2,1,0:T(8,128)(2,1)S(1)}, u32[]{:S(2)}, u32[]{:S(2)}) collective-permute-start(bf16[32,16,128]{2,1,0:T(8,128)(2,1)S(1)} %get-tuple-element.50), channel_id=1, source_target_pairs={{0,14},{2,0},{4,2},{6,4},{8,6},{10,8},{12,10},{14,12},{1,15},{3,1}... | collective-permute-start | bytes 393224 | tf_op jit(solution)/shard_map/ppermute | solution.py:394
  234.3 22.8 %copy-start.3 = (f32[512,16,128]{2,1,0:T(8,128)S(1)}, f32[512,16,128]{2,1,0:T(8,128)}, u32[]{:S(2)}) copy-start(f32[512,16,128]{2,1,0:T(8,128)} %copy-done.2) | copy-start | bytes 12582916
  252.8 4.2 %collective-permute-start.10 = (bf16[512,16,128]{2,1,0:T(8,128)(2,1)S(1)}, bf16[512,16,128]{2,1,0:T(8,128)(2,1)S(1)}, u32[]{:S(2)}, u32[]{:S(2)}) collective-permute-start(bf16[512,16,128]{2,1,0:T(8,128)(2,1)S(1)} %get-tuple-element.42), channel_id=1, source_target_pairs={{0,1},{1,0},{2,3},{3,2},{4,5},{5,4},{6,7},{7,6},{8,9},{9,8},{10,11... | collective-permute-start | bytes 6291464 | tf_op jit(solution)/shard_map/ppermute | solution.py:377
  253.1 5.7 %copy-start.5 = (bf16[8,32,16,128]{3,2,1,0:T(8,128)(2,1)}, bf16[8,32,16,128]{3,2,1,0:T(8,128)(2,1)S(1)}, u32[]{:S(2)}) copy-start(bf16[8,32,16,128]{3,2,1,0:T(8,128)(2,1)S(1)} %bitcast_dynamic-update-slice_fusion.early_ref) | copy-start | bytes 3145732

commit v4 on v3

--- a/solution.py
+++ b/solution.py
@@ -13,10 +13,19 @@
 ANY = pl.BlockSpec(memory_space=pl.ANY)
 
 
+def flipped(index, bits, devices):
+    total, unit = index, 1
+    while unit < devices:
+        if bits & unit:
+            total = total + unit * (1 - 2 * lax.rem(index // unit, 2))
+        unit *= 2
+    return total
+
+
 def spread_kernel(
-    nrow, stored, parcel, names, diag,
+    nrow, stored, target, names, diag,
     tiles, field, all_names, all_diag,
-    ring_send, ring_recv, send, recv, own_sem,
+    parcel, ring_send, ring_recv, send, recv, own_sem,
 ):
     devices = 2 * nrow
     row, col, core = lax.axis_index("row"), lax.axis_index("col"), lax.axis_index("rhs")
@@ -64,13 +73,20 @@
         return copy
 
     now = [hop(lane, 0) for lane in range(lanes)]
+
+    def pack(b, carry):
+        low = target[b].astype(jnp.bfloat16).T
+        parcel[:, b] = low.reshape(devices, parcel.shape[2], parcel.shape[3])
+        return carry
+
+    lax.fori_loop(0, target.shape[0], pack, 0)
     straight = []
     pairs = ((names, all_names, False), (diag, all_diag, False), (parcel, field, True))
-    for n, (source, target, apart) in enumerate(pairs):
+    for n, (source, whole, apart) in enumerate(pairs):
         for offset in range(1, devices):
             copy = pltpu.make_async_remote_copy(
                 src_ref=source.at[lax.rem(me + offset, devices)] if apart else source,
-                dst_ref=target.at[me],
+                dst_ref=whole.at[me],
                 send_sem=send.at[n, offset - 1],
                 recv_sem=recv.at[n, offset - 1],
                 device_id=peer(offset),
@@ -85,8 +101,8 @@
         (diag, all_diag.at[me]),
         (parcel.at[me], field.at[me]),
     )
-    for n, (source, target) in enumerate(owns):
-        copy = pltpu.make_async_copy(source, target, own_sem.at[n])
+    for n, (source, whole) in enumerate(owns):
+        copy = pltpu.make_async_copy(source, whole, own_sem.at[n])
         copy.start()
         local.append(copy)
     for step in range(1, devices):
@@ -104,22 +120,24 @@
         copy.wait()
 
 
-def spread(stored, parcel, names, diag):
+def spread(stored, target, names, diag):
     nrow = lax.axis_size("row")
     devices = 2 * nrow
     half, cores, width, _ = stored.shape
+    parcel = (devices, target.shape[0], target.shape[2] // devices, target.shape[1])
     lanes = 6 if half % 6 == 0 else 2
     return pl.pallas_call(
         functools.partial(spread_kernel, nrow),
         out_shape=(
             jax.ShapeDtypeStruct((devices, half, width, width), stored.dtype),
-            jax.ShapeDtypeStruct(parcel.shape, parcel.dtype),
+            jax.ShapeDtypeStruct(parcel, jnp.bfloat16),
             jax.ShapeDtypeStruct((devices,) + names.shape, names.dtype),
             jax.ShapeDtypeStruct((devices,) + diag.shape, diag.dtype),
         ),
-        in_specs=[ANY] * 4,
+        in_specs=[ANY, pl.BlockSpec(memory_space=pltpu.VMEM), ANY, ANY],
         out_specs=[ANY] * 4,
         scratch_shapes=[
+            pltpu.VMEM(parcel, jnp.bfloat16),
             pltpu.SemaphoreType.DMA((lanes, devices - 1)),
             pltpu.SemaphoreType.DMA((lanes, devices - 1)),
             pltpu.SemaphoreType.DMA((3, devices - 1)),
@@ -127,15 +145,15 @@
             pltpu.SemaphoreType.DMA((4,)),
         ],
         compiler_params=pltpu.CompilerParams(collective_id=0, has_side_effects=True),
-    )(stored, parcel, names, diag)
+    )(stored, target, names, diag)
 
 
 def home_kernel(nrow, early, first, parcel, scale, late, field, scales, send, recv, own_sem):
     devices = 2 * nrow
     me = lax.axis_index("row") * 2 + lax.axis_index("col")
 
-    def peer(offset):
-        other = lax.rem(me + offset, devices)
+    def peer(bits):
+        other = flipped(me, bits, devices)
         return {"row": other // 2, "col": lax.rem(other, 2)}
 
     barrier = pltpu.get_barrier_semaphore()
@@ -143,13 +161,21 @@
         pl.semaphore_signal(barrier, inc=1, device_id=peer(offset), device_id_type=MESH)
     pl.semaphore_wait(barrier, devices - 1)
     copies = []
-    rest = pl.ds(early, late.shape[1])
-    for n, target in enumerate((scales, late, field)):
+    rest = pl.ds(early, late.shape[1] - early)
+    for n in range(3):
         for offset in range(1, devices):
-            to = lax.rem(me + offset, devices)
+            to = flipped(me, offset, devices)
+            if n == 0:
+                source, target = scale, scales.at[me]
+            elif n == 2:
+                source, target = parcel.at[to], field.at[me]
+            elif offset < devices // 2:
+                source, target = first.at[to], late.at[me]
+            else:
+                source, target = first.at[to, rest], late.at[me, rest]
             copy = pltpu.make_async_remote_copy(
-                src_ref=(scale, first.at[to, rest], parcel.at[to])[n],
-                dst_ref=target.at[me],
+                src_ref=source,
+                dst_ref=target,
                 send_sem=send.at[n, offset - 1],
                 recv_sem=recv.at[n, offset - 1],
                 device_id=peer(offset),
@@ -159,7 +185,7 @@
             copies.append(copy)
     owns = (
         (scale, scales.at[me]),
-        (first.at[me, rest], late.at[me]),
+        (first.at[me], late.at[me]),
         (parcel.at[me], field.at[me]),
     )
     for n, (source, target) in enumerate(owns):
@@ -172,11 +198,11 @@
 
 def send_home(first, parcel, scale, early):
     nrow = lax.axis_size("row")
-    devices, blocks = parcel.shape[:2]
+    devices = parcel.shape[0]
     return pl.pallas_call(
         functools.partial(home_kernel, nrow, early),
         out_shape=(
-            jax.ShapeDtypeStruct((devices, blocks - early) + parcel.shape[2:], parcel.dtype),
+            jax.ShapeDtypeStruct(parcel.shape, parcel.dtype),
             jax.ShapeDtypeStruct(parcel.shape, parcel.dtype),
             jax.ShapeDtypeStruct((devices,) + scale.shape, scale.dtype),
         ),
@@ -191,47 +217,24 @@
     )(first, parcel, scale)
 
 
-def pack_kernel(target_ref, parcel_ref):
-    devices, blocks, own, width = parcel_ref.shape
-    for b in range(blocks):
-        low = target_ref[b].T.astype(jnp.bfloat16)
-        parcel_ref[:, b] = low.reshape(devices, own, width)
-
-
-def pack(target, devices):
-    blocks, width, columns = target.shape
-    own = columns // devices
-    step = min(8, blocks)
-    return pl.pallas_call(
-        pack_kernel,
-        out_shape=jax.ShapeDtypeStruct((devices, blocks, own, width), jnp.bfloat16),
-        grid=(blocks // step,),
-        in_specs=[pl.BlockSpec((step, width, columns), lambda g: (g, 0, 0))],
-        out_specs=pl.BlockSpec((devices, step, own, width), lambda g: (0, g, 0, 0)),
-    )(target)
-
-
 def finish_kernel(me_ref, target_ref, diag_ref, early_ref, late_ref, second_ref, scale_ref,
                   answer_ref, residual_ref, first_ref):
     blocks, width, columns = target_ref.shape
     alpha1, alpha2, beta = scale_ref[0:1], scale_ref[1:2], scale_ref[2:3]
     devices = second_ref.shape[0]
-    late = pl.program_id(0) >= pl.num_programs(0) // 2
-
-    @pl.when(late)
+    first_ref[...] = late_ref[...]
+
+    @pl.when(pl.program_id(0) < pl.num_programs(0) // 2)
     def _():
-        first_ref[...] = late_ref[...]
-
-    @pl.when(jnp.logical_not(late))
-    def _():
-        for source in range(devices):
-            first_ref[source] = early_ref[lax.rem(me_ref[0] - source + devices, devices)]
-
+        for far in range(devices // 2):
+            first_ref[me_ref[0] ^ (devices // 2 + far)] = early_ref[far]
+
+    diags = diag_ref[...].T
     for b in range(blocks):
         target = target_ref[b]
-        diag = jnp.transpose(jnp.broadcast_to(diag_ref[pl.ds(b, 1), :], (columns, width)))
-        first = first_ref[:, b].reshape(columns, width).astype(jnp.float32).T
-        second = second_ref[:, b].reshape(columns, width).astype(jnp.float32).T
+        diag = diags[:, b : b + 1]
+        first = first_ref[:, b].reshape(columns, width).T.astype(jnp.float32)
+        second = second_ref[:, b].reshape(columns, width).T.astype(jnp.float32)
         lost = target - target.astype(jnp.bfloat16).astype(jnp.float32)
         lost1 = lost - alpha1 * diag * lost
         answer_ref[b] = alpha1 * target + alpha2 * (first + lost1 + beta * target)
@@ -253,8 +256,8 @@
             pl.BlockSpec(memory_space=pltpu.SMEM),
             whole,
             pl.BlockSpec((step, width), lambda g: (g, 0)),
-            pl.BlockSpec((devices, step, own, width), lambda g: (0, jnp.minimum(g, last - 1), 0, 0)),
-            pl.BlockSpec((devices, step, own, width), lambda g: (0, jnp.maximum(g - last, 0), 0, 0)),
+            pl.BlockSpec(early.shape[:1] + (step, own, width), lambda g: (0, jnp.minimum(g, last - 1), 0, 0)),
+            part,
             part,
             pl.BlockSpec(scales.shape, lambda g: (0, 0)),
         ],
@@ -361,7 +364,7 @@
     target_blocks = target.reshape(quarter, width, target.shape[1])
 
     tiles, field, all_names, all_diag = spread(
-        stored.reshape(half, 2, width, width), pack(target_blocks, devices), names, diag_own
+        stored.reshape(half, 2, width, width), target_blocks, names, diag_own
     )
     all_names = all_names.reshape(devices, -1)
     irows = all_names[:, :half].reshape(-1)
@@ -385,14 +388,11 @@
     def parcels(value):
         return value.astype(jnp.bfloat16).reshape(devices, quarter, own, width)
 
-    def home_by_offset(parcel):
+    def far_home(parcel):
         pieces = []
-        for offset in range(devices):
-            piece = lax.dynamic_index_in_dim(parcel, (me + offset) % devices, 0, keepdims=False)
-            if offset:
-                pairs = [(d, (d + offset) % devices) for d in range(devices)]
-                piece = lax.ppermute(piece, grid, pairs)
-            pieces.append(piece)
+        for bits in range(devices // 2, devices):
+            piece = lax.dynamic_index_in_dim(parcel, me ^ bits, 0, keepdims=False)
+            pieces.append(lax.ppermute(piece, grid, [(d, d ^ bits) for d in range(devices)]))
         return pieces
 
     low = field.reshape(-1, own, width)
@@ -406,7 +406,7 @@
     direction = first + beta * start
     first_parcel = parcels(first)
     early = quarter // 2
-    pieces = home_by_offset(first_parcel[:, :early])
+    pieces = far_home(first_parcel[:, :early])
     image, pieces = image_of(direction, direction.astype(jnp.bfloat16), pieces)
     first_early = jnp.stack(pieces)
     alpha2 = norm1 / inner(direction, image)
@@ -434,6 +434,7 @@
     if (
         nrow * ncol * tile_bytes <= GATHER_BYTES
         and ncol == 2
+        and nrow & (nrow - 1) == 0
         and lax.axis_size("rhs") == 2
         and target.shape[1] == 16 * nrow * ncol
         and blocks.shape[2] % (2 * UNROLL) == 0

time: 361 us -> 340 us (0.942)
  Pallas kernels: 310 us -> 297 us
  starting transfers between devices: 12.7 us -> 6.33 us
    pallas_call x1, Pallas kernels: 82.8 us -> 74 us  [send_home(): pl.pallas_call(functools.partial(home_kernel, nrow, early), out_shape=(ja...]
    pallas_call x1 -> x0, Pallas kernels: 6.52 us -> none  [pack(): pl.pallas_call(pack_kernel, out_shape=jax.ShapeDtypeStruct((devices, bloc...]
    ppermute x7 -> x4, starting transfers between devices: 12.3 us -> 5.92 us  [far_home(): lax.ppermute(piece, grid, [(d, d ^ bits) for d in range(devices)])]
  transfers between devices with their start and end apart: 11 -> 8, of which waited for: 4 -> 4; matrix products, arithmetic and copies ran while one was open for 1% -> 1% of each run, Pallas kernels for 5% -> 5%
where the time goes in v4:
time: 340 us; the launch traced here: 338 us
  Pallas kernels  297 us (87%)
  other arithmetic  14.5 us (4%)
  waiting for transfers between devices  10.7 us (3%)
  local copies, waits for them, and re-layouts  7.67 us (2%)
  starting transfers between devices  6.33 us (2%)
    pallas_call x1, Pallas kernels, spread(): pl.pallas_call(functools.partial(spread_kernel, nrow), out_shape=(jax.Sha...  178 us
    pallas_call x1, Pallas kernels, send_home(): pl.pallas_call(functools.partial(home_kernel, nrow, early), out_shape=(ja...  74 us
    pallas_call x2, Pallas kernels, operate(): pl.pallas_call(functools.partial(operate_kernel, slots), out_shape=(jax.S...  35.2 us
    pallas_call x1, Pallas kernels, finish(): pl.pallas_call(finish_kernel, out_shape=(jax.ShapeDtypeStruct(target.shap...  10.7 us
  transfers between devices with their start and end apart: 8, of which 4 were waited for; matrix products, arithmetic and copies ran while one was open for 1% of the time, Pallas kernels for 5%

profile of v4, /device:TPU:12, one launch (start us, length us, event | category | flops | bytes accessed | tf_op | source)
XLA Modules:
  0.0 338.1 jit_solution(8024854718906016825)
XLA Ops:
  1.3 0.7 fusion.5
  2.0 0.1 slice.29
  2.1 0.1 slice.30
  2.2 0.7 add_bitcast_fusion
  2.9 0.1 slice.27
  3.0 0.1 slice.28
  3.2 0.1 pad_add_fusion
  3.3 0.6 pad_bitcast_fusion.names
  3.9 177.6 %shard_map.77 = (bf16[8,48,128,128]{3,2,1,0:T(8,128)(2,1)}, bf16[8,64,16,128]{3,2,1,0:T(8,128)(2,1)}, s32[8,8,128]{2,1,0:T(8,128)}, f32[8,64,128]{2,1,0:T(8,128)}) custom-call(bf16[48,2,128,128]{3,2,1,0:T(8,128)(2,1)} %bitcast.74, f32[64,128,128]{2,1,0:T(8,128)} %bitcast.65, s32[8,128]{1,0:T(8,128)} %pad_bitcast_fusion.names, f32[64,128]{1,0:T(8,128)} %bitcast.75), custom_call_target="tpu_custom_call" | custom-call | tf_op jit(solution)/shard_map/pallas_call | solution.py:129
  181.5 0.1 collective-permute-start
  181.6 0.8 copy.15
  182.3 0.1 slice.38
  182.4 0.1 fusion.7
  182.5 0.1 reshape.113.irow_ref
  182.5 0.1 reshape.114.icol_ref
  182.6 0.1 copy.11
  182.7 3.2 collective-permute-done.theirs_ref
  185.9 1.6 copy-done
  187.5 16.9 %shard_map.78 = (f32[512,16,128]{2,1,0:T(8,128)S(1)}, bf16[512,16,128]{2,1,0:T(8,128)(2,1)S(1)}) custom-call(s32[384]{0:T(512)S(1)} %reshape.113.irow_ref, s32[384]{0:T(512)S(1)} %reshape.114.icol_ref, s32[8]{0:T(128)S(1)} %bitcast.63, bf16[8,48,128,128]{3,2,1,0:T(8,128)(2,1)} %get-tuple-element.22.blocks_ref, bf16[512,16,128]{2,1,0:T(8,128)(2,1)S(1)} %bitcast.62, ...), custom_call_target="tpu_custom_call" | custom-call | flops 3221225472 | bytes 62914560 | tf_op jit(solution)/shard_map/pallas_call | solution.py:317
  204.4 0.2 collective-permute-start.1
  204.6 0.7 multiply_reduce_fusion.2
  205.2 3.4 collective-permute-done.1
  208.6 1.3 fusion.2
  209.9 0.3 copy-done.1
  210.2 2.6 fusion.6
  212.8 0.7 multiply_reduce_fusion.1
  213.5 2.0 fusion.4.mine_ref
  215.5 0.1 collective-permute-start.2
  215.6 1.4 slice.39
  217.1 0.1 collective-permute-start.3
  217.2 2.9 collective-permute-start.4
  220.1 1.5 collective-permute-start.5
  221.6 1.5 collective-permute-start.6
  223.0 0.0 collective-permute-done.2.theirs_ref
  223.0 18.4 %shard_map.79 = (f32[512,16,128]{2,1,0:T(8,128)S(1)}, bf16[512,16,128]{2,1,0:T(8,128)(2,1)S(1)}) custom-call(s32[384]{0:T(512)S(1)} %reshape.113.irow_ref, s32[384]{0:T(512)S(1)} %reshape.114.icol_ref, s32[8]{0:T(128)S(1)} %bitcast.64, bf16[8,48,128,128]{3,2,1,0:T(8,128)(2,1)} %get-tuple-element.22.blocks_ref, bf16[512,16,128]{2,1,0:T(8,128)(2,1)} %fusion.4.mine_ref, ...), custom_call_target="tpu_custom_call" | custom-call | flops 3221225472 | bytes 62914560 | tf_op jit(solution)/shard_map/pallas_call | solution.py:317
  241.4 0.0 collective-permute-done.3
  241.4 0.0 collective-permute-done.4
  241.5 0.9 collective-permute-done.6
  242.3 0.0 collective-permute-start.7
  242.3 0.9 pad_maximum_fusion.early_ref
  243.2 3.3 collective-permute-done.7
  246.5 1.8 multiply_reduce_fusion
  248.4 0.6 pad.9.scale
  249.0 3.0 subtract_convert_fusion
  252.0 74.0 %shard_map.80 = (bf16[8,64,16,128]{3,2,1,0:T(8,128)(2,1)}, bf16[8,64,16,128]{3,2,1,0:T(8,128)(2,1)}, f32[8,8,128]{2,1,0:T(8,128)}) custom-call(bf16[8,64,16,128]{3,2,1,0:T(8,128)(2,1)} %bitcast.68, bf16[8,64,16,128]{3,2,1,0:T(8,128)(2,1)} %bitcast.69, f32[8,128]{1,0:T(8,128)} %pad.9.scale), custom_call_target="tpu_custom_call" | custom-call | tf_op jit(solution)/shard_map/pallas_call | solution.py:202
  326.0 0.8 slice_bitcast_fusion
  326.8 0.7 reshape.119.scale_ref
  327.4 10.7 %shard_map.81 = (f32[64,128,128]{2,1,0:T(8,128)}, f32[64,128,128]{2,1,0:T(8,128)}) custom-call(s32[1]{0:T(128)} %bitcast.me_ref, f32[64,128,128]{2,1,0:T(8,128)} %bitcast.66, f32[64,128]{1,0:T(8,128)} %bitcast.76, bf16[4,32,16,128]{3,2,1,0:T(8,128)(2,1)} %pad_maximum_fusion.early_ref, bf16[8,64,16,128]{3,2,1,0:T(8,128)(2,1)} %get-tuple-element.35.late_ref, ...), custom_call_target="tpu_custom_call" | custom-call | tf_op jit(solution)/shard_map/pallas_call | solution.py:251
  (17 shorter events, 0.1 us)
Async XLA Ops:
  181.5 4.4 %collective-permute-start = (bf16[512,16,128]{2,1,0:T(8,128)(2,1)}, bf16[512,16,128]{2,1,0:T(8,128)(2,1)S(1)}, u32[]{:S(2)}, u32[]{:S(2)}) collective-permute-start(bf16[512,16,128]{2,1,0:T(8,128)(2,1)} %bitcast.61), channel_id=1, source_target_pairs={{0,1},{1,0},{2,3},{3,2},{4,5},{5,4},{6,7},{7,6},{8,9},{9,8},{10,11... | collective-permute-start | bytes 6291464 | tf_op jit(solution)/shard_map/ppermute | solution.py:377
  185.9 1.6 copy-start
  187.5 21.1 %copy-start.4 = (f32[8,64,128]{2,1,0:T(8,128)S(1)}, f32[8,64,128]{2,1,0:T(8,128)}, u32[]{:S(2)}) copy-start(f32[8,64,128]{2,1,0:T(8,128)} %get-tuple-element.24) | copy-start | bytes 786436
  204.4 4.2 %collective-permute-start.1 = (bf16[512,16,128]{2,1,0:T(8,128)(2,1)S(1)}, bf16[512,16,128]{2,1,0:T(8,128)(2,1)S(1)}, u32[]{:S(2)}, u32[]{:S(2)}) collective-permute-start(bf16[512,16,128]{2,1,0:T(8,128)(2,1)S(1)} %get-tuple-element.26), channel_id=1, source_target_pairs={{0,1},{1,0},{2,3},{3,2},{4,5},{5,4},{6,7},{7,6},{8,9},{9,8},{10,11... | collective-permute-start | bytes 6291464 | tf_op jit(solution)/shard_map/ppermute | solution.py:380
  208.6 1.6 copy-start.1
  212.8 2.7 copy-start.2
  215.5 7.5 %collective-permute-start.2 = (bf16[512,16,128]{2,1,0:T(8,128)(2,1)}, bf16[512,16,128]{2,1,0:T(8,128)(2,1)}, u32[]{:S(2)}, u32[]{:S(2)}) collective-permute-start(bf16[512,16,128]{2,1,0:T(8,128)(2,1)} %fusion.4.mine_ref), channel_id=1, source_target_pairs={{0,1},{1,0},{2,3},{3,2},{4,5},{5,4},{6,7},{7,6},{8,9},{9,8},{10,11... | collective-permute-start | bytes 6291464 | tf_op jit(solution)/shard_map/ppermute | solution.py:377
  217.1 24.3 %collective-permute-start.3 = (bf16[32,16,128]{2,1,0:T(8,128)(2,1)S(1)}, bf16[32,16,128]{2,1,0:T(8,128)(2,1)S(1)}, u32[]{:S(2)}, u32[]{:S(2)}) collective-permute-start(bf16[32,16,128]{2,1,0:T(8,128)(2,1)S(1)} %get-tuple-element.45), channel_id=1, source_target_pairs={{0,8},{2,10},{4,12},{6,14},{8,0},{10,2},{12,4},{14,6},{1,9},{3,11}... | collective-permute-start | bytes 393224 | tf_op jit(solution)/shard_map/ppermute | solution.py:395
  217.2 24.3 %collective-permute-start.4 = (bf16[32,16,128]{2,1,0:T(8,128)(2,1)S(1)}, bf16[32,16,128]{2,1,0:T(8,128)(2,1)S(1)}, u32[]{:S(2)}, u32[]{:S(2)}) collective-permute-start(bf16[32,16,128]{2,1,0:T(8,128)(2,1)S(1)} %get-tuple-element.44), channel_id=1, source_target_pairs={{0,10},{2,8},{4,14},{6,12},{8,2},{10,0},{12,6},{14,4},{1,11},{3,9}... | collective-permute-start | bytes 393224 | tf_op jit(solution)/shard_map/ppermute | solution.py:395
  220.1 21.4 %collective-permute-start.5 = (bf16[32,16,128]{2,1,0:T(8,128)(2,1)S(1)}, bf16[32,16,128]{2,1,0:T(8,128)(2,1)S(1)}, u32[]{:S(2)}, u32[]{:S(2)}) collective-permute-start(bf16[32,16,128]{2,1,0:T(8,128)(2,1)S(1)} %get-tuple-element.43), channel_id=1, source_target_pairs={{0,12},{2,14},{4,8},{6,10},{8,4},{10,6},{12,0},{14,2},{1,13},{3,15... | collective-permute-start | bytes 393224 | tf_op jit(solution)/shard_map/ppermute | solution.py:395
  221.6 24.9 %copy-start.3 = (f32[512,16,128]{2,1,0:T(8,128)S(1)}, f32[512,16,128]{2,1,0:T(8,128)}, u32[]{:S(2)}) copy-start(f32[512,16,128]{2,1,0:T(8,128)} %copy-done.2) | copy-start | bytes 12582916
  221.6 20.8 %collective-permute-start.6 = (bf16[32,16,128]{2,1,0:T(8,128)(2,1)S(1)}, bf16[32,16,128]{2,1,0:T(8,128)(2,1)S(1)}, u32[]{:S(2)}, u32[]{:S(2)}) collective-permute-start(bf16[32,16,128]{2,1,0:T(8,128)(2,1)S(1)} %get-tuple-element.42), channel_id=1, source_target_pairs={{0,14},{2,12},{4,10},{6,8},{8,6},{10,4},{12,2},{14,0},{1,15},{3,13... | collective-permute-start | bytes 393224 | tf_op jit(solution)/shard_map/ppermute | solution.py:395
  242.3 4.2 %collective-permute-start.7 = (bf16[512,16,128]{2,1,0:T(8,128)(2,1)S(1)}, bf16[512,16,128]{2,1,0:T(8,128)(2,1)S(1)}, u32[]{:S(2)}, u32[]{:S(2)}) collective-permute-start(bf16[512,16,128]{2,1,0:T(8,128)(2,1)S(1)} %get-tuple-element.34), channel_id=1, source_target_pairs={{0,1},{1,0},{2,3},{3,2},{4,5},{5,4},{6,7},{7,6},{8,9},{9,8},{10,11... | collective-permute-start | bytes 6291464 | tf_op jit(solution)/shard_map/ppermute | solution.py:380

commit v5 on v4

--- a/solution.py
+++ b/solution.py
@@ -24,8 +24,8 @@
 
 def spread_kernel(
     nrow, stored, target, names, diag,
-    tiles, field, all_names, all_diag,
-    parcel, ring_send, ring_recv, send, recv, own_sem,
+    tiles, field, theirs, all_names, all_diag,
+    parcel, ring_send, ring_recv, send, recv, own_sem, pair_sem,
 ):
     devices = 2 * nrow
     row, col, core = lax.axis_index("row"), lax.axis_index("col"), lax.axis_index("rhs")
@@ -44,7 +44,9 @@
     barrier = pltpu.get_barrier_semaphore()
     for offset in range(1, devices):
         pl.semaphore_signal(barrier, inc=1, device_id=peer(offset), device_id_type=MESH)
-    pl.semaphore_wait(barrier, devices - 1)
+    sibling = {"rhs": 1 - core}
+    pl.semaphore_signal(barrier, inc=1, device_id=sibling, device_id_type=MESH)
+    pl.semaphore_wait(barrier, devices)
 
     half = tiles.shape[1]
     lanes = ring_send.shape[0]
@@ -106,6 +108,20 @@
         copy.start()
         local.append(copy)
     for step in range(1, devices):
+        if step == devices - 1:
+            for copy in straight:
+                copy.wait()
+            for copy in local:
+                copy.wait()
+            pair = pltpu.make_async_remote_copy(
+                src_ref=field,
+                dst_ref=theirs,
+                send_sem=pair_sem.at[0],
+                recv_sem=pair_sem.at[1],
+                device_id=sibling,
+                device_id_type=MESH,
+            )
+            pair.start()
         for lane in range(lanes):
             now[lane].wait_recv()
             if step < devices - 1:
@@ -114,10 +130,7 @@
     hops += now
     for copy in hops:
         copy.wait_send()
-    for copy in straight:
-        copy.wait()
-    for copy in local:
-        copy.wait()
+    pair.wait()
 
 
 def spread(stored, target, names, diag):
@@ -131,11 +144,12 @@
         out_shape=(
             jax.ShapeDtypeStruct((devices, half, width, width), stored.dtype),
             jax.ShapeDtypeStruct(parcel, jnp.bfloat16),
+            jax.ShapeDtypeStruct(parcel, jnp.bfloat16),
             jax.ShapeDtypeStruct((devices,) + names.shape, names.dtype),
             jax.ShapeDtypeStruct((devices,) + diag.shape, diag.dtype),
         ),
         in_specs=[ANY, pl.BlockSpec(memory_space=pltpu.VMEM), ANY, ANY],
-        out_specs=[ANY] * 4,
+        out_specs=[ANY] * 5,
         scratch_shapes=[
             pltpu.VMEM(parcel, jnp.bfloat16),
             pltpu.SemaphoreType.DMA((lanes, devices - 1)),
@@ -143,6 +157,7 @@
             pltpu.SemaphoreType.DMA((3, devices - 1)),
             pltpu.SemaphoreType.DMA((3, devices - 1)),
             pltpu.SemaphoreType.DMA((4,)),
+            pltpu.SemaphoreType.DMA((2,)),
         ],
         compiler_params=pltpu.CompilerParams(collective_id=0, has_side_effects=True),
     )(stored, target, names, diag)
@@ -217,14 +232,14 @@
     )(first, parcel, scale)
 
 
-def finish_kernel(me_ref, target_ref, diag_ref, early_ref, late_ref, second_ref, scale_ref,
+def finish_kernel(last, me_ref, target_ref, diag_ref, early_ref, late_ref, second_ref, scale_ref,
                   answer_ref, residual_ref, first_ref):
     blocks, width, columns = target_ref.shape
     alpha1, alpha2, beta = scale_ref[0:1], scale_ref[1:2], scale_ref[2:3]
     devices = second_ref.shape[0]
     first_ref[...] = late_ref[...]
 
-    @pl.when(pl.program_id(0) < pl.num_programs(0) // 2)
+    @pl.when(pl.program_id(0) < last)
     def _():
         for far in range(devices // 2):
             first_ref[me_ref[0] ^ (devices // 2 + far)] = early_ref[far]
@@ -244,12 +259,12 @@
 def finish(me, target, diag, early, late, second, scales):
     blocks, width, columns = target.shape
     devices, _, own, _ = second.shape
-    step = min(8, blocks // 2)
-    last = blocks // step // 2
+    step = 8
+    last = early.shape[1] // step
     whole = pl.BlockSpec((step, width, columns), lambda g: (g, 0, 0))
     part = pl.BlockSpec((devices, step, own, width), lambda g: (0, g, 0, 0))
     return pl.pallas_call(
-        finish_kernel,
+        functools.partial(finish_kernel, last),
         out_shape=(jax.ShapeDtypeStruct(target.shape, jnp.float32),) * 2,
         grid=(blocks // step,),
         in_specs=[
@@ -363,7 +378,7 @@
     diag_own = diagonal.reshape(quarter, width)
     target_blocks = target.reshape(quarter, width, target.shape[1])
 
-    tiles, field, all_names, all_diag = spread(
+    tiles, field, field_pair, all_names, all_diag = spread(
         stored.reshape(half, 2, width, width), target_blocks, names, diag_own
     )
     all_names = all_names.reshape(devices, -1)
@@ -373,12 +388,11 @@
     diag = all_diag.reshape(-1, 1, width)
     swap = [(0, 1), (1, 0)]
 
-    def image_of(direction, low, beside=()):
-        theirs = lax.ppermute(low, "rhs", swap)
+    def image_of(direction, low, theirs, beside=()):
         here, away = operate(tiles, irows, icols, used, low, theirs)
         (here, away), beside = lax.optimization_barrier(((here, away), beside))
-        away = lax.ppermute(away, "rhs", swap).astype(jnp.float32)
-        return diag * direction + here + away, beside
+        away = lax.ppermute(away, "rhs", swap)
+        return diag * direction + here + away.astype(jnp.float32), beside
 
     def inner(a, b):
         return jnp.sum(a * b, axis=(0, 2), keepdims=True)
@@ -398,16 +412,17 @@
     low = field.reshape(-1, own, width)
     start = low.astype(jnp.float32)
     norm0 = inner(start, start)
-    image, _ = image_of(start, low)
+    image, _ = image_of(start, low, field_pair.reshape(low.shape))
     alpha1 = norm0 / inner(start, image)
     first = start - alpha1 * image
     norm1 = inner(first, first)
     beta = norm1 / norm0
     direction = first + beta * start
     first_parcel = parcels(first)
-    early = quarter // 2
+    early = quarter // 8 * 5
     pieces = far_home(first_parcel[:, :early])
-    image, pieces = image_of(direction, direction.astype(jnp.bfloat16), pieces)
+    low = direction.astype(jnp.bfloat16)
+    image, pieces = image_of(direction, low, lax.ppermute(low, "rhs", swap), pieces)
     first_early = jnp.stack(pieces)
     alpha2 = norm1 / inner(direction, image)
     second = first - alpha2 * image
@@ -438,7 +453,7 @@
         and lax.axis_size("rhs") == 2
         and target.shape[1] == 16 * nrow * ncol
         and blocks.shape[2] % (2 * UNROLL) == 0
-        and target.shape[0] // blocks.shape[3] % 16 == 0
+        and target.shape[0] // blocks.shape[3] % 64 == 0
     ):
         return by_columns(blocks, block_rows, block_cols, counts, diagonal, target)
     stored = blocks[0, 0]

time: 340 us -> 336 us (0.988)
  Pallas kernels: 297 us -> 292 us
    pallas_call x1, Pallas kernels: 74 us -> 67.2 us  [send_home(): pl.pallas_call(functools.partial(home_kernel, nrow, early), out_shape=(ja...]
    ppermute x4, waiting for transfers between devices: 0.87 us -> 5.87 us  [far_home(): lax.ppermute(piece, grid, [(d, d ^ bits) for d in range(devices)])]
    ppermute x4 -> x3, waiting for transfers between devices: 9.85 us -> 6.71 us  [the longest x2 6.7 us: image_of(): away = lax.ppermute(away, 'rhs', swap)]
  transfers between devices with their start and end apart: 8 -> 7, of which waited for: 4 -> 4; matrix products, arithmetic and copies ran while one was open for 1% -> 1% of each run, Pallas kernels for 5% -> 6%
where the time goes in v5:
time: 336 us
  Pallas kernels  292 us (87%)
  other arithmetic  14.5 us (4%)
  waiting for transfers between devices  12.6 us (4%)
  local copies, waits for them, and re-layouts  9.47 us (3%)
  starting transfers between devices  6.13 us (2%)
    pallas_call x1, Pallas kernels, spread(): pl.pallas_call(functools.partial(spread_kernel, nrow), out_shape=(jax.Sha...  178 us
    pallas_call x1, Pallas kernels, send_home(): pl.pallas_call(functools.partial(home_kernel, nrow, early), out_shape=(ja...  67.2 us
    pallas_call x2, Pallas kernels, operate(): pl.pallas_call(functools.partial(operate_kernel, slots), out_shape=(jax.S...  36.2 us
    pallas_call x1, Pallas kernels, finish(): pl.pallas_call(functools.partial(finish_kernel, last), out_shape=(jax.Sha...  10.8 us
  transfers between devices with their start and end apart: 7, of which 4 were waited for; matrix products, arithmetic and copies ran while one was open for 1% of the time, Pallas kernels for 6%

profile of v5, /device:TPU:12, one launch (start us, length us, event | category | flops | bytes accessed | tf_op | source)
XLA Modules:
  0.0 335.9 jit_solution(5371389786722921047)
XLA Ops:
  1.3 0.7 fusion.5
  2.0 0.1 slice.29
  2.1 0.1 slice.30
  2.2 0.7 add_bitcast_fusion
  2.9 0.1 slice.27
  3.0 0.1 slice.28
  3.2 0.1 pad_add_fusion
  3.3 0.6 pad_bitcast_fusion.names
  3.9 177.5 %shard_map.77 = (bf16[8,48,128,128]{3,2,1,0:T(8,128)(2,1)}, bf16[8,64,16,128]{3,2,1,0:T(8,128)(2,1)}, bf16[8,64,16,128]{3,2,1,0:T(8,128)(2,1)}, s32[8,8,128]{2,1,0:T(8,128)}, f32[8,64,128]{2,1,0:T(8,128)}) custom-call(bf16[48,2,128,128]{3,2,1,0:T(8,128)(2,1)} %bitcast.75, f32[64,128,128]{2,1,0:T(8,128)} %bitcast.66, s32[8,128]{1,0:T(8,128)} %pad_bitcast_fusion.names, ...), custom_call_target="tpu_custom_call" | custom-call | tf_op jit(solution)/shard_map/pallas_call | solution.py:142
  181.4 0.8 copy.15
  182.2 0.1 fusion.7
  182.3 0.1 slice.38
  182.3 0.1 reshape.116.irow_ref
  182.4 0.1 reshape.117.icol_ref
  182.5 0.1 copy.11
  182.6 1.6 copy-done
  184.2 1.6 copy-done.2
  185.8 17.2 %shard_map.78 = (f32[512,16,128]{2,1,0:T(8,128)S(1)}, bf16[512,16,128]{2,1,0:T(8,128)(2,1)S(1)}) custom-call(s32[384]{0:T(512)S(1)} %reshape.116.irow_ref, s32[384]{0:T(512)S(1)} %reshape.117.icol_ref, s32[8]{0:T(128)S(1)} %bitcast.64, bf16[8,48,128,128]{3,2,1,0:T(8,128)(2,1)} %get-tuple-element.23.blocks_ref, bf16[512,16,128]{2,1,0:T(8,128)(2,1)S(1)} %bitcast.62, ...), custom_call_target="tpu_custom_call" | custom-call | flops 3221225472 | bytes 62914560 | tf_op jit(solution)/shard_map/pallas_call | solution.py:332
  203.0 0.1 collective-permute-start
  203.0 0.7 multiply_reduce_fusion.2
  203.7 3.5 %collective-permute-done = bf16[512,16,128]{2,1,0:T(8,128)(2,1)S(1)} collective-permute-done((bf16[512,16,128]{2,1,0:T(8,128)(2,1)S(1)}, bf16[512,16,128]{2,1,0:T(8,128)(2,1)S(1)}, u32[]{:S(2)}, u32[]{:S(2)}) %collective-permute-start) | collective-permute-done | bytes 2097184 | tf_op jit(solution)/shard_map/ppermute | solution.py:394
  207.2 1.3 fusion.2
  208.5 0.3 copy-done.1
  208.8 2.6 fusion.6
  211.4 0.7 multiply_reduce_fusion.1
  212.1 2.0 fusion.4.mine_ref
  214.1 0.1 collective-permute-start.1
  214.2 1.5 slice.39
  215.8 0.1 dynamic-slice_bitcast_fusion
  215.9 0.1 collective-permute-start.2
  216.0 2.9 collective-permute-start.3
  218.9 1.5 collective-permute-start.4
  220.4 1.5 collective-permute-start.5
  221.8 0.0 collective-permute-done.1.theirs_ref
  221.9 19.0 %shard_map.79 = (f32[512,16,128]{2,1,0:T(8,128)S(1)}, bf16[512,16,128]{2,1,0:T(8,128)(2,1)S(1)}) custom-call(s32[384]{0:T(512)S(1)} %reshape.116.irow_ref, s32[384]{0:T(512)S(1)} %reshape.117.icol_ref, s32[8]{0:T(128)S(1)} %bitcast.65, bf16[8,48,128,128]{3,2,1,0:T(8,128)(2,1)} %get-tuple-element.23.blocks_ref, bf16[512,16,128]{2,1,0:T(8,128)(2,1)} %fusion.4.mine_ref, ...), custom_call_target="tpu_custom_call" | custom-call | flops 3221225472 | bytes 62914560 | tf_op jit(solution)/shard_map/pallas_call | solution.py:332
  240.9 0.0 collective-permute-done.2
  240.9 2.7 collective-permute-done.4
  243.6 3.1 collective-permute-done.5
  246.8 0.0 collective-permute-start.6
  246.8 0.9 pad_maximum_fusion.early_ref
  247.7 3.2 collective-permute-done.6
  250.9 1.8 multiply_reduce_fusion
  252.8 0.6 pad.9.scale
  253.4 3.0 subtract_convert_fusion
  256.4 67.2 %shard_map.80 = (bf16[8,64,16,128]{3,2,1,0:T(8,128)(2,1)}, bf16[8,64,16,128]{3,2,1,0:T(8,128)(2,1)}, f32[8,8,128]{2,1,0:T(8,128)}) custom-call(bf16[8,64,16,128]{3,2,1,0:T(8,128)(2,1)} %bitcast.69, bf16[8,64,16,128]{3,2,1,0:T(8,128)(2,1)} %bitcast.70, f32[8,128]{1,0:T(8,128)} %pad.9.scale), custom_call_target="tpu_custom_call" | custom-call | tf_op jit(solution)/shard_map/pallas_call | solution.py:217
  323.6 0.8 slice_bitcast_fusion
  324.4 0.7 reshape.123.scale_ref
  325.0 10.8 %shard_map.81 = (f32[64,128,128]{2,1,0:T(8,128)}, f32[64,128,128]{2,1,0:T(8,128)}) custom-call(s32[1]{0:T(128)} %bitcast.me_ref, f32[64,128,128]{2,1,0:T(8,128)} %bitcast.67, f32[64,128]{1,0:T(8,128)} %bitcast.81, bf16[4,40,16,128]{3,2,1,0:T(8,128)(2,1)} %pad_maximum_fusion.early_ref, bf16[8,64,16,128]{3,2,1,0:T(8,128)(2,1)} %get-tuple-element.37.late_ref, ...), custom_call_target="tpu_custom_call" | custom-call | tf_op jit(solution)/shard_map/pallas_call | solution.py:266
  (17 shorter events, 0.1 us)
Async XLA Ops:
  182.6 1.6 copy-start
  184.2 1.6 copy-start.2
  185.8 21.4 %copy-start.5 = (f32[8,64,128]{2,1,0:T(8,128)S(1)}, f32[8,64,128]{2,1,0:T(8,128)}, u32[]{:S(2)}) copy-start(f32[8,64,128]{2,1,0:T(8,128)} %get-tuple-element.25) | copy-start | bytes 786436
  203.0 4.2 %collective-permute-start = (bf16[512,16,128]{2,1,0:T(8,128)(2,1)S(1)}, bf16[512,16,128]{2,1,0:T(8,128)(2,1)S(1)}, u32[]{:S(2)}, u32[]{:S(2)}) collective-permute-start(bf16[512,16,128]{2,1,0:T(8,128)(2,1)S(1)} %get-tuple-element.28), channel_id=1, source_target_pairs={{0,1},{1,0},{2,3},{3,2},{4,5},{5,4},{6,7},{7,6},{8,9},{9,8},{10,11... | collective-permute-start | bytes 6291464 | tf_op jit(solution)/shard_map/ppermute | solution.py:394
  207.2 1.6 copy-start.1
  211.4 2.7 copy-start.3
  214.1 7.7 %collective-permute-start.1 = (bf16[512,16,128]{2,1,0:T(8,128)(2,1)}, bf16[512,16,128]{2,1,0:T(8,128)(2,1)}, u32[]{:S(2)}, u32[]{:S(2)}) collective-permute-start(bf16[512,16,128]{2,1,0:T(8,128)(2,1)} %fusion.4.mine_ref), channel_id=1, source_target_pairs={{0,1},{1,0},{2,3},{3,2},{4,5},{5,4},{6,7},{7,6},{8,9},{9,8},{10,11... | collective-permute-start | bytes 6291464 | tf_op jit(solution)/shard_map/ppermute | solution.py:425
  215.9 25.0 %collective-permute-start.2 = (bf16[40,16,128]{2,1,0:T(8,128)(2,1)S(1)}, bf16[40,16,128]{2,1,0:T(8,128)(2,1)S(1)}, u32[]{:S(2)}, u32[]{:S(2)}) collective-permute-start(bf16[40,16,128]{2,1,0:T(8,128)(2,1)S(1)} %get-tuple-element.47), channel_id=1, source_target_pairs={{0,8},{2,10},{4,12},{6,14},{8,0},{10,2},{12,4},{14,6},{1,9},{3,11}... | collective-permute-start | bytes 491528 | tf_op jit(solution)/shard_map/ppermute | solution.py:409
  216.0 24.9 %collective-permute-start.3 = (bf16[40,16,128]{2,1,0:T(8,128)(2,1)S(1)}, bf16[40,16,128]{2,1,0:T(8,128)(2,1)S(1)}, u32[]{:S(2)}, u32[]{:S(2)}) collective-permute-start(bf16[40,16,128]{2,1,0:T(8,128)(2,1)S(1)} %get-tuple-element.46), channel_id=1, source_target_pairs={{0,10},{2,8},{4,14},{6,12},{8,2},{10,0},{12,6},{14,4},{1,11},{3,9}... | collective-permute-start | bytes 491528 | tf_op jit(solution)/shard_map/ppermute | solution.py:409
  218.9 24.8 %collective-permute-start.4 = (bf16[40,16,128]{2,1,0:T(8,128)(2,1)S(1)}, bf16[40,16,128]{2,1,0:T(8,128)(2,1)S(1)}, u32[]{:S(2)}, u32[]{:S(2)}) collective-permute-start(bf16[40,16,128]{2,1,0:T(8,128)(2,1)S(1)} %get-tuple-element.45), channel_id=1, source_target_pairs={{0,12},{2,14},{4,8},{6,10},{8,4},{10,6},{12,0},{14,2},{1,13},{3,15... | collective-permute-start | bytes 491528 | tf_op jit(solution)/shard_map/ppermute | solution.py:409
  220.4 26.4 %collective-permute-start.5 = (bf16[40,16,128]{2,1,0:T(8,128)(2,1)S(1)}, bf16[40,16,128]{2,1,0:T(8,128)(2,1)S(1)}, u32[]{:S(2)}, u32[]{:S(2)}) collective-permute-start(bf16[40,16,128]{2,1,0:T(8,128)(2,1)S(1)} %get-tuple-element.44), channel_id=1, source_target_pairs={{0,14},{2,12},{4,10},{6,8},{8,6},{10,4},{12,2},{14,0},{1,15},{3,13... | collective-permute-start | bytes 491528 | tf_op jit(solution)/shard_map/ppermute | solution.py:409
  221.9 29.1 %copy-start.4 = (f32[512,16,128]{2,1,0:T(8,128)S(1)}, f32[512,16,128]{2,1,0:T(8,128)}, u32[]{:S(2)}) copy-start(f32[512,16,128]{2,1,0:T(8,128)} %copy-done.3) | copy-start | bytes 12582916
  246.8 4.2 %collective-permute-start.6 = (bf16[512,16,128]{2,1,0:T(8,128)(2,1)S(1)}, bf16[512,16,128]{2,1,0:T(8,128)(2,1)S(1)}, u32[]{:S(2)}, u32[]{:S(2)}) collective-permute-start(bf16[512,16,128]{2,1,0:T(8,128)(2,1)S(1)} %get-tuple-element.36), channel_id=1, source_target_pairs={{0,1},{1,0},{2,3},{3,2},{4,5},{5,4},{6,7},{7,6},{8,9},{9,8},{10,11... | collective-permute-start | bytes 6291464 | tf_op jit(solution)/shard_map/ppermute | solution.py:394

commit v6 on v5

--- a/solution.py
+++ b/solution.py
@@ -138,7 +138,7 @@
     devices = 2 * nrow
     half, cores, width, _ = stored.shape
     parcel = (devices, target.shape[0], target.shape[2] // devices, target.shape[1])
-    lanes = 6 if half % 6 == 0 else 2
+    lanes = 12 if half % 12 == 0 else 2
     return pl.pallas_call(
         functools.partial(spread_kernel, nrow),
         out_shape=(

time: 336 us -> 338 us (level)
  no operation moved by 1% of the time
where the time goes in v6:
time: 338 us; the launch traced here: 337 us
  Pallas kernels  293 us (87%)
  other arithmetic  14.5 us (4%)
  waiting for transfers between devices  12.6 us (4%)
  local copies, waits for them, and re-layouts  9.47 us (3%)
  starting transfers between devices  6.13 us (2%)
    pallas_call x1, Pallas kernels, spread(): pl.pallas_call(functools.partial(spread_kernel, nrow), out_shape=(jax.Sha...  178 us
    pallas_call x1, Pallas kernels, send_home(): pl.pallas_call(functools.partial(home_kernel, nrow, early), out_shape=(ja...  67.2 us
    pallas_call x2, Pallas kernels, operate(): pl.pallas_call(functools.partial(operate_kernel, slots), out_shape=(jax.S...  36.2 us
    pallas_call x1, Pallas kernels, finish(): pl.pallas_call(functools.partial(finish_kernel, last), out_shape=(jax.Sha...  10.8 us
  transfers between devices with their start and end apart: 7, of which 4 were waited for; matrix products, arithmetic and copies ran while one was open for 1% of the time, Pallas kernels for 6%

profile of v6, /device:TPU:12, one launch (start us, length us, event | category | flops | bytes accessed | tf_op | source)
XLA Modules:
  0.0 336.7 jit_solution(50444869391909228)
XLA Ops:
  1.3 0.7 fusion.5
  2.0 0.1 slice.29
  2.1 0.1 slice.30
  2.2 0.7 add_bitcast_fusion
  2.9 0.1 slice.27
  3.0 0.1 slice.28
  3.2 0.1 pad_add_fusion
  3.3 0.6 pad_bitcast_fusion.names
  3.9 178.3 %shard_map.77 = (bf16[8,48,128,128]{3,2,1,0:T(8,128)(2,1)}, bf16[8,64,16,128]{3,2,1,0:T(8,128)(2,1)}, bf16[8,64,16,128]{3,2,1,0:T(8,128)(2,1)}, s32[8,8,128]{2,1,0:T(8,128)}, f32[8,64,128]{2,1,0:T(8,128)}) custom-call(bf16[48,2,128,128]{3,2,1,0:T(8,128)(2,1)} %bitcast.75, f32[64,128,128]{2,1,0:T(8,128)} %bitcast.66, s32[8,128]{1,0:T(8,128)} %pad_bitcast_fusion.names, ...), custom_call_target="tpu_custom_call" | custom-call | tf_op jit(solution)/shard_map/pallas_call | solution.py:142
  182.2 0.8 copy.15
  183.0 0.1 fusion.7
  183.1 0.1 slice.38
  183.2 0.1 reshape.116.irow_ref
  183.2 0.1 reshape.117.icol_ref
  183.3 0.1 copy.11
  183.4 1.6 copy-done
  185.0 1.6 copy-done.2
  186.6 17.2 %shard_map.78 = (f32[512,16,128]{2,1,0:T(8,128)S(1)}, bf16[512,16,128]{2,1,0:T(8,128)(2,1)S(1)}) custom-call(s32[384]{0:T(512)S(1)} %reshape.116.irow_ref, s32[384]{0:T(512)S(1)} %reshape.117.icol_ref, s32[8]{0:T(128)S(1)} %bitcast.64, bf16[8,48,128,128]{3,2,1,0:T(8,128)(2,1)} %get-tuple-element.23.blocks_ref, bf16[512,16,128]{2,1,0:T(8,128)(2,1)S(1)} %bitcast.62, ...), custom_call_target="tpu_custom_call" | custom-call | flops 3221225472 | bytes 62914560 | tf_op jit(solution)/shard_map/pallas_call | solution.py:332
  203.8 0.1 collective-permute-start
  203.9 0.7 multiply_reduce_fusion.2
  204.5 3.5 %collective-permute-done = bf16[512,16,128]{2,1,0:T(8,128)(2,1)S(1)} collective-permute-done((bf16[512,16,128]{2,1,0:T(8,128)(2,1)S(1)}, bf16[512,16,128]{2,1,0:T(8,128)(2,1)S(1)}, u32[]{:S(2)}, u32[]{:S(2)}) %collective-permute-start) | collective-permute-done | bytes 2097184 | tf_op jit(solution)/shard_map/ppermute | solution.py:394
  208.0 1.3 fusion.2
  209.3 0.3 copy-done.1
  209.6 2.6 fusion.6
  212.2 0.7 multiply_reduce_fusion.1
  212.9 2.0 fusion.4.mine_ref
  214.9 0.1 collective-permute-start.1
  215.1 1.5 slice.39
  216.6 0.1 dynamic-slice_bitcast_fusion
  216.8 0.1 collective-permute-start.2
  216.8 2.9 collective-permute-start.3
  219.7 1.5 collective-permute-start.4
  221.2 1.5 collective-permute-start.5
  222.7 0.0 collective-permute-done.1.theirs_ref
  222.7 19.0 %shard_map.79 = (f32[512,16,128]{2,1,0:T(8,128)S(1)}, bf16[512,16,128]{2,1,0:T(8,128)(2,1)S(1)}) custom-call(s32[384]{0:T(512)S(1)} %reshape.116.irow_ref, s32[384]{0:T(512)S(1)} %reshape.117.icol_ref, s32[8]{0:T(128)S(1)} %bitcast.65, bf16[8,48,128,128]{3,2,1,0:T(8,128)(2,1)} %get-tuple-element.23.blocks_ref, bf16[512,16,128]{2,1,0:T(8,128)(2,1)} %fusion.4.mine_ref, ...), custom_call_target="tpu_custom_call" | custom-call | flops 3221225472 | bytes 62914560 | tf_op jit(solution)/shard_map/pallas_call | solution.py:332
  241.7 0.0 collective-permute-done.2
  241.7 2.8 collective-permute-done.4
  244.5 3.1 collective-permute-done.5
  247.6 0.0 collective-permute-start.6
  247.6 0.9 pad_maximum_fusion.early_ref
  248.5 3.2 collective-permute-done.6
  251.8 1.8 multiply_reduce_fusion
  253.6 0.6 pad.9.scale
  254.2 3.0 subtract_convert_fusion
  257.2 67.2 %shard_map.80 = (bf16[8,64,16,128]{3,2,1,0:T(8,128)(2,1)}, bf16[8,64,16,128]{3,2,1,0:T(8,128)(2,1)}, f32[8,8,128]{2,1,0:T(8,128)}) custom-call(bf16[8,64,16,128]{3,2,1,0:T(8,128)(2,1)} %bitcast.69, bf16[8,64,16,128]{3,2,1,0:T(8,128)(2,1)} %bitcast.70, f32[8,128]{1,0:T(8,128)} %pad.9.scale), custom_call_target="tpu_custom_call" | custom-call | tf_op jit(solution)/shard_map/pallas_call | solution.py:217
  324.4 0.8 slice_bitcast_fusion
  325.2 0.7 reshape.123.scale_ref
  325.9 10.8 %shard_map.81 = (f32[64,128,128]{2,1,0:T(8,128)}, f32[64,128,128]{2,1,0:T(8,128)}) custom-call(s32[1]{0:T(128)} %bitcast.me_ref, f32[64,128,128]{2,1,0:T(8,128)} %bitcast.67, f32[64,128]{1,0:T(8,128)} %bitcast.81, bf16[4,40,16,128]{3,2,1,0:T(8,128)(2,1)} %pad_maximum_fusion.early_ref, bf16[8,64,16,128]{3,2,1,0:T(8,128)(2,1)} %get-tuple-element.37.late_ref, ...), custom_call_target="tpu_custom_call" | custom-call | tf_op jit(solution)/shard_map/pallas_call | solution.py:266
  (17 shorter events, 0.1 us)
Async XLA Ops:
  183.4 1.6 copy-start
  185.0 1.6 copy-start.2
  186.6 21.4 %copy-start.5 = (f32[8,64,128]{2,1,0:T(8,128)S(1)}, f32[8,64,128]{2,1,0:T(8,128)}, u32[]{:S(2)}) copy-start(f32[8,64,128]{2,1,0:T(8,128)} %get-tuple-element.25) | copy-start | bytes 786436
  203.8 4.2 %collective-permute-start = (bf16[512,16,128]{2,1,0:T(8,128)(2,1)S(1)}, bf16[512,16,128]{2,1,0:T(8,128)(2,1)S(1)}, u32[]{:S(2)}, u32[]{:S(2)}) collective-permute-start(bf16[512,16,128]{2,1,0:T(8,128)(2,1)S(1)} %get-tuple-element.28), channel_id=1, source_target_pairs={{0,1},{1,0},{2,3},{3,2},{4,5},{5,4},{6,7},{7,6},{8,9},{9,8},{10,11... | collective-permute-start | bytes 6291464 | tf_op jit(solution)/shard_map/ppermute | solution.py:394
  208.0 1.6 copy-start.1
  212.2 2.7 copy-start.3
  214.9 7.7 %collective-permute-start.1 = (bf16[512,16,128]{2,1,0:T(8,128)(2,1)}, bf16[512,16,128]{2,1,0:T(8,128)(2,1)}, u32[]{:S(2)}, u32[]{:S(2)}) collective-permute-start(bf16[512,16,128]{2,1,0:T(8,128)(2,1)} %fusion.4.mine_ref), channel_id=1, source_target_pairs={{0,1},{1,0},{2,3},{3,2},{4,5},{5,4},{6,7},{7,6},{8,9},{9,8},{10,11... | collective-permute-start | bytes 6291464 | tf_op jit(solution)/shard_map/ppermute | solution.py:425
  216.8 25.0 %collective-permute-start.2 = (bf16[40,16,128]{2,1,0:T(8,128)(2,1)S(1)}, bf16[40,16,128]{2,1,0:T(8,128)(2,1)S(1)}, u32[]{:S(2)}, u32[]{:S(2)}) collective-permute-start(bf16[40,16,128]{2,1,0:T(8,128)(2,1)S(1)} %get-tuple-element.47), channel_id=1, source_target_pairs={{0,8},{2,10},{4,12},{6,14},{8,0},{10,2},{12,4},{14,6},{1,9},{3,11}... | collective-permute-start | bytes 491528 | tf_op jit(solution)/shard_map/ppermute | solution.py:409
  216.8 24.9 %collective-permute-start.3 = (bf16[40,16,128]{2,1,0:T(8,128)(2,1)S(1)}, bf16[40,16,128]{2,1,0:T(8,128)(2,1)S(1)}, u32[]{:S(2)}, u32[]{:S(2)}) collective-permute-start(bf16[40,16,128]{2,1,0:T(8,128)(2,1)S(1)} %get-tuple-element.46), channel_id=1, source_target_pairs={{0,10},{2,8},{4,14},{6,12},{8,2},{10,0},{12,6},{14,4},{1,11},{3,9}... | collective-permute-start | bytes 491528 | tf_op jit(solution)/shard_map/ppermute | solution.py:409
  219.7 24.8 %collective-permute-start.4 = (bf16[40,16,128]{2,1,0:T(8,128)(2,1)S(1)}, bf16[40,16,128]{2,1,0:T(8,128)(2,1)S(1)}, u32[]{:S(2)}, u32[]{:S(2)}) collective-permute-start(bf16[40,16,128]{2,1,0:T(8,128)(2,1)S(1)} %get-tuple-element.45), channel_id=1, source_target_pairs={{0,12},{2,14},{4,8},{6,10},{8,4},{10,6},{12,0},{14,2},{1,13},{3,15... | collective-permute-start | bytes 491528 | tf_op jit(solution)/shard_map/ppermute | solution.py:409
  221.2 26.4 %collective-permute-start.5 = (bf16[40,16,128]{2,1,0:T(8,128)(2,1)S(1)}, bf16[40,16,128]{2,1,0:T(8,128)(2,1)S(1)}, u32[]{:S(2)}, u32[]{:S(2)}) collective-permute-start(bf16[40,16,128]{2,1,0:T(8,128)(2,1)S(1)} %get-tuple-element.44), channel_id=1, source_target_pairs={{0,14},{2,12},{4,10},{6,8},{8,6},{10,4},{12,2},{14,0},{1,15},{3,13... | collective-permute-start | bytes 491528 | tf_op jit(solution)/shard_map/ppermute | solution.py:409
  222.7 29.1 %copy-start.4 = (f32[512,16,128]{2,1,0:T(8,128)S(1)}, f32[512,16,128]{2,1,0:T(8,128)}, u32[]{:S(2)}) copy-start(f32[512,16,128]{2,1,0:T(8,128)} %copy-done.3) | copy-start | bytes 12582916
  247.6 4.2 %collective-permute-start.6 = (bf16[512,16,128]{2,1,0:T(8,128)(2,1)S(1)}, bf16[512,16,128]{2,1,0:T(8,128)(2,1)S(1)}, u32[]{:S(2)}, u32[]{:S(2)}) collective-permute-start(bf16[512,16,128]{2,1,0:T(8,128)(2,1)S(1)} %get-tuple-element.36), channel_id=1, source_target_pairs={{0,1},{1,0},{2,3},{3,2},{4,5},{5,4},{6,7},{7,6},{8,9},{9,8},{10,11... | collective-permute-start | bytes 6291464 | tf_op jit(solution)/shard_map/ppermute | solution.py:394

commit v7 on v6

--- a/solution.py
+++ b/solution.py
@@ -7,7 +7,7 @@
 from jax.sharding import PartitionSpec as P
 
 ITERS = 2
-UNROLL = 8
+UNROLL = 4
 GATHER_BYTES = 32 * 2**20
 MESH = pl.DeviceIdType.MESH
 ANY = pl.BlockSpec(memory_space=pl.ANY)

time: 338 us -> 343 us (1.015)
  Pallas kernels: 293 us -> 303 us
  waiting for transfers between devices: 12.6 us -> 7.57 us
    pallas_call x2, Pallas kernels: 36.2 us -> 46.2 us  [operate(): pl.pallas_call(functools.partial(operate_kernel, slots), out_shape=(jax.S...]
    ppermute x4, waiting for transfers between devices: 5.87 us -> 0.87 us  [far_home(): lax.ppermute(piece, grid, [(d, d ^ bits) for d in range(devices)])]
  transfers between devices with their start and end apart: 7 -> 7, of which waited for: 4 -> 3; matrix products, arithmetic and copies ran while one was open for 1% -> 1% of each run, Pallas kernels for 6% -> 7%
where the time goes in v7:
time: 343 us; the launch traced here: 342 us
  Pallas kernels  303 us (88%)
  other arithmetic  14.5 us (4%)
  local copies, waits for them, and re-layouts  9.47 us (3%)
  waiting for transfers between devices  7.57 us (2%)
  starting transfers between devices  6.13 us (2%)
    pallas_call x1, Pallas kernels, spread(): pl.pallas_call(functools.partial(spread_kernel, nrow), out_shape=(jax.Sha...  178 us
    pallas_call x1, Pallas kernels, send_home(): pl.pallas_call(functools.partial(home_kernel, nrow, early), out_shape=(ja...  67.7 us
    pallas_call x2, Pallas kernels, operate(): pl.pallas_call(functools.partial(operate_kernel, slots), out_shape=(jax.S...  46.2 us
    pallas_call x1, Pallas kernels, finish(): pl.pallas_call(functools.partial(finish_kernel, last), out_shape=(jax.Sha...  10.8 us
  transfers between devices with their start and end apart: 7, of which 3 were waited for; matrix products, arithmetic and copies ran while one was open for 1% of the time, Pallas kernels for 7%

profile of v7, /device:TPU:12, one launch (start us, length us, event | category | flops | bytes accessed | tf_op | source)
XLA Modules:
  0.0 342.2 jit_solution(2616160838774171641)
XLA Ops:
  1.3 0.7 fusion.5
  2.0 0.1 slice.29
  2.1 0.1 slice.30
  2.2 0.7 add_bitcast_fusion
  2.9 0.1 slice.27
  3.0 0.1 slice.28
  3.2 0.1 pad_add_fusion
  3.3 0.6 pad_bitcast_fusion.names
  3.9 178.3 %shard_map.77 = (bf16[8,48,128,128]{3,2,1,0:T(8,128)(2,1)}, bf16[8,64,16,128]{3,2,1,0:T(8,128)(2,1)}, bf16[8,64,16,128]{3,2,1,0:T(8,128)(2,1)}, s32[8,8,128]{2,1,0:T(8,128)}, f32[8,64,128]{2,1,0:T(8,128)}) custom-call(bf16[48,2,128,128]{3,2,1,0:T(8,128)(2,1)} %bitcast.75, f32[64,128,128]{2,1,0:T(8,128)} %bitcast.66, s32[8,128]{1,0:T(8,128)} %pad_bitcast_fusion.names, ...), custom_call_target="tpu_custom_call" | custom-call | tf_op jit(solution)/shard_map/pallas_call | solution.py:142
  182.2 0.8 copy.15
  183.0 0.1 fusion.7
  183.1 0.1 slice.38
  183.2 0.1 reshape.116.irow_ref
  183.2 0.1 reshape.117.icol_ref
  183.3 0.1 copy.11
  183.4 1.6 copy-done
  185.0 1.6 copy-done.2
  186.6 22.2 %shard_map.78 = (f32[512,16,128]{2,1,0:T(8,128)S(1)}, bf16[512,16,128]{2,1,0:T(8,128)(2,1)S(1)}) custom-call(s32[384]{0:T(512)S(1)} %reshape.116.irow_ref, s32[384]{0:T(512)S(1)} %reshape.117.icol_ref, s32[8]{0:T(128)S(1)} %bitcast.64, bf16[8,48,128,128]{3,2,1,0:T(8,128)(2,1)} %get-tuple-element.23.blocks_ref, bf16[512,16,128]{2,1,0:T(8,128)(2,1)S(1)} %bitcast.62, ...), custom_call_target="tpu_custom_call" | custom-call | flops 3221225472 | bytes 62914560 | tf_op jit(solution)/shard_map/pallas_call | solution.py:332
  208.8 0.1 collective-permute-start
  208.8 0.7 multiply_reduce_fusion.2
  209.5 3.5 %collective-permute-done = bf16[512,16,128]{2,1,0:T(8,128)(2,1)S(1)} collective-permute-done((bf16[512,16,128]{2,1,0:T(8,128)(2,1)S(1)}, bf16[512,16,128]{2,1,0:T(8,128)(2,1)S(1)}, u32[]{:S(2)}, u32[]{:S(2)}) %collective-permute-start) | collective-permute-done | bytes 2097184 | tf_op jit(solution)/shard_map/ppermute | solution.py:394
  213.0 1.3 fusion.2
  214.3 0.3 copy-done.1
  214.6 2.6 fusion.6
  217.2 0.7 multiply_reduce_fusion.1
  217.9 2.0 fusion.4.mine_ref
  219.9 0.1 collective-permute-start.1
  220.0 1.5 slice.39
  221.6 0.1 dynamic-slice_bitcast_fusion
  221.7 0.1 collective-permute-start.2
  221.8 2.9 collective-permute-start.3
  224.7 1.5 collective-permute-start.4
  226.2 1.5 collective-permute-start.5
  227.6 0.0 collective-permute-done.1.theirs_ref
  227.7 24.0 %shard_map.79 = (f32[512,16,128]{2,1,0:T(8,128)S(1)}, bf16[512,16,128]{2,1,0:T(8,128)(2,1)S(1)}) custom-call(s32[384]{0:T(512)S(1)} %reshape.116.irow_ref, s32[384]{0:T(512)S(1)} %reshape.117.icol_ref, s32[8]{0:T(128)S(1)} %bitcast.65, bf16[8,48,128,128]{3,2,1,0:T(8,128)(2,1)} %get-tuple-element.23.blocks_ref, bf16[512,16,128]{2,1,0:T(8,128)(2,1)} %fusion.4.mine_ref, ...), custom_call_target="tpu_custom_call" | custom-call | flops 3221225472 | bytes 62914560 | tf_op jit(solution)/shard_map/pallas_call | solution.py:332
  251.7 0.0 collective-permute-done.3
  251.7 0.0 collective-permute-done.4
  251.7 0.9 collective-permute-done.5
  252.6 0.0 collective-permute-start.6
  252.6 0.9 pad_maximum_fusion.early_ref
  253.5 3.2 collective-permute-done.6
  256.7 1.8 multiply_reduce_fusion
  258.6 0.6 pad.9.scale
  259.2 3.0 subtract_convert_fusion
  262.2 67.7 %shard_map.80 = (bf16[8,64,16,128]{3,2,1,0:T(8,128)(2,1)}, bf16[8,64,16,128]{3,2,1,0:T(8,128)(2,1)}, f32[8,8,128]{2,1,0:T(8,128)}) custom-call(bf16[8,64,16,128]{3,2,1,0:T(8,128)(2,1)} %bitcast.69, bf16[8,64,16,128]{3,2,1,0:T(8,128)(2,1)} %bitcast.70, f32[8,128]{1,0:T(8,128)} %pad.9.scale), custom_call_target="tpu_custom_call" | custom-call | tf_op jit(solution)/shard_map/pallas_call | solution.py:217
  329.9 0.8 slice_bitcast_fusion
  330.7 0.7 reshape.123.scale_ref
  331.4 10.8 %shard_map.81 = (f32[64,128,128]{2,1,0:T(8,128)}, f32[64,128,128]{2,1,0:T(8,128)}) custom-call(s32[1]{0:T(128)} %bitcast.me_ref, f32[64,128,128]{2,1,0:T(8,128)} %bitcast.67, f32[64,128]{1,0:T(8,128)} %bitcast.81, bf16[4,40,16,128]{3,2,1,0:T(8,128)(2,1)} %pad_maximum_fusion.early_ref, bf16[8,64,16,128]{3,2,1,0:T(8,128)(2,1)} %get-tuple-element.37.late_ref, ...), custom_call_target="tpu_custom_call" | custom-call | tf_op jit(solution)/shard_map/pallas_call | solution.py:266
  (17 shorter events, 0.1 us)
Async XLA Ops:
  183.4 1.6 copy-start
  185.0 1.6 copy-start.2
  186.6 26.4 %copy-start.5 = (f32[8,64,128]{2,1,0:T(8,128)S(1)}, f32[8,64,128]{2,1,0:T(8,128)}, u32[]{:S(2)}) copy-start(f32[8,64,128]{2,1,0:T(8,128)} %get-tuple-element.25) | copy-start | bytes 786436
  208.8 4.2 %collective-permute-start = (bf16[512,16,128]{2,1,0:T(8,128)(2,1)S(1)}, bf16[512,16,128]{2,1,0:T(8,128)(2,1)S(1)}, u32[]{:S(2)}, u32[]{:S(2)}) collective-permute-start(bf16[512,16,128]{2,1,0:T(8,128)(2,1)S(1)} %get-tuple-element.28), channel_id=1, source_target_pairs={{0,1},{1,0},{2,3},{3,2},{4,5},{5,4},{6,7},{7,6},{8,9},{9,8},{10,11... | collective-permute-start | bytes 6291464 | tf_op jit(solution)/shard_map/ppermute | solution.py:394
  213.0 1.6 copy-start.1
  217.2 2.7 copy-start.3
  219.9 7.7 %collective-permute-start.1 = (bf16[512,16,128]{2,1,0:T(8,128)(2,1)}, bf16[512,16,128]{2,1,0:T(8,128)(2,1)}, u32[]{:S(2)}, u32[]{:S(2)}) collective-permute-start(bf16[512,16,128]{2,1,0:T(8,128)(2,1)} %fusion.4.mine_ref), channel_id=1, source_target_pairs={{0,1},{1,0},{2,3},{3,2},{4,5},{5,4},{6,7},{7,6},{8,9},{9,8},{10,11... | collective-permute-start | bytes 6291464 | tf_op jit(solution)/shard_map/ppermute | solution.py:425
  221.7 30.0 %collective-permute-start.2 = (bf16[40,16,128]{2,1,0:T(8,128)(2,1)S(1)}, bf16[40,16,128]{2,1,0:T(8,128)(2,1)S(1)}, u32[]{:S(2)}, u32[]{:S(2)}) collective-permute-start(bf16[40,16,128]{2,1,0:T(8,128)(2,1)S(1)} %get-tuple-element.47), channel_id=1, source_target_pairs={{0,8},{2,10},{4,12},{6,14},{8,0},{10,2},{12,4},{14,6},{1,9},{3,11}... | collective-permute-start | bytes 491528 | tf_op jit(solution)/shard_map/ppermute | solution.py:409
  221.8 29.9 %collective-permute-start.3 = (bf16[40,16,128]{2,1,0:T(8,128)(2,1)S(1)}, bf16[40,16,128]{2,1,0:T(8,128)(2,1)S(1)}, u32[]{:S(2)}, u32[]{:S(2)}) collective-permute-start(bf16[40,16,128]{2,1,0:T(8,128)(2,1)S(1)} %get-tuple-element.46), channel_id=1, source_target_pairs={{0,10},{2,8},{4,14},{6,12},{8,2},{10,0},{12,6},{14,4},{1,11},{3,9}... | collective-permute-start | bytes 491528 | tf_op jit(solution)/shard_map/ppermute | solution.py:409
  224.7 27.0 %collective-permute-start.4 = (bf16[40,16,128]{2,1,0:T(8,128)(2,1)S(1)}, bf16[40,16,128]{2,1,0:T(8,128)(2,1)S(1)}, u32[]{:S(2)}, u32[]{:S(2)}) collective-permute-start(bf16[40,16,128]{2,1,0:T(8,128)(2,1)S(1)} %get-tuple-element.45), channel_id=1, source_target_pairs={{0,12},{2,14},{4,8},{6,10},{8,4},{10,6},{12,0},{14,2},{1,13},{3,15... | collective-permute-start | bytes 491528 | tf_op jit(solution)/shard_map/ppermute | solution.py:409
  226.2 26.4 %collective-permute-start.5 = (bf16[40,16,128]{2,1,0:T(8,128)(2,1)S(1)}, bf16[40,16,128]{2,1,0:T(8,128)(2,1)S(1)}, u32[]{:S(2)}, u32[]{:S(2)}) collective-permute-start(bf16[40,16,128]{2,1,0:T(8,128)(2,1)S(1)} %get-tuple-element.44), channel_id=1, source_target_pairs={{0,14},{2,12},{4,10},{6,8},{8,6},{10,4},{12,2},{14,0},{1,15},{3,13... | collective-permute-start | bytes 491528 | tf_op jit(solution)/shard_map/ppermute | solution.py:409
  227.7 29.1 %copy-start.4 = (f32[512,16,128]{2,1,0:T(8,128)S(1)}, f32[512,16,128]{2,1,0:T(8,128)}, u32[]{:S(2)}) copy-start(f32[512,16,128]{2,1,0:T(8,128)} %copy-done.3) | copy-start | bytes 12582916
  252.6 4.2 %collective-permute-start.6 = (bf16[512,16,128]{2,1,0:T(8,128)(2,1)S(1)}, bf16[512,16,128]{2,1,0:T(8,128)(2,1)S(1)}, u32[]{:S(2)}, u32[]{:S(2)}) collective-permute-start(bf16[512,16,128]{2,1,0:T(8,128)(2,1)S(1)} %get-tuple-element.36), channel_id=1, source_target_pairs={{0,1},{1,0},{2,3},{3,2},{4,5},{5,4},{6,7},{7,6},{8,9},{9,8},{10,11... | collective-permute-start | bytes 6291464 | tf_op jit(solution)/shard_map/ppermute | solution.py:394
